TPU v7x, 256 devices: a whole 4x4x8 slice. The times are simulated.
256 devices in a mesh: seq: 32 (over y, z), head: 8 (over x, core).
Axes of the slice: x: 4, y: 4, z: 8, core: 2. Of those that a mesh axis runs over, the one named last changes fastest.
Arguments:
- query: bfloat16 [16384, 2048], P('seq', 'head'), may hold values from -6 to 6
- keys: bfloat16 [16384, 2048], P('seq', 'head'), may hold values from -6 to 6
- values: bfloat16 [16384, 4096], P('seq', 'head'), may hold values from -6 to 6
- gate_logit: float32 [16384, 32], P('seq', 'head'), may hold values from -17 to 1.5
- beta_logit: float32 [16384, 32], P('seq', 'head'), may hold values from -9 to 6
- decay_rate: float32 [32], P('head'), may hold values from 0.5 to 8
- norm_gain: float32 [128], replicated, may hold values from 0.1 to 1.9
- gate_z: bfloat16 [16384, 4096], P('seq', 'head'), may hold values from -6 to 6
- out_weight: bfloat16 [4096, 2048], P('head'), may hold values from -0.09375 to 0.09375
Outputs:
- mixed: bfloat16 [16384, 2048], P(('seq', 'head'))
All inputs are finite; a program needn't handle non-finite values.
Results may differ from a plain program's by a relative error of at most 0.014.
Values may be sent and summed in bfloat16 or wider, within the bound.
A program may use at most 128 MiB of HBM per device.

v0:
```python
import jax
import jax.numpy as jnp
from jax import lax
from jax.sharding import PartitionSpec as P

DK = 128
DV = 128
SPAN = 64


def passed_along(shard, axis, by):
    size = lax.axis_size(axis)
    pairs = [(i, i + by) for i in range(size) if 0 <= i + by < size]
    return lax.ppermute(shard, axis, pairs)


def unit_norm(values_in):
    return values_in * lax.rsqrt(jnp.sum(values_in * values_in, axis=-1, keepdims=True) + 1e-06)


def block_terms(query, keys, values, logdecay, beta):
    highest = lax.Precision.HIGHEST
    size = logdecay.shape[-1]
    width = keys.shape[-1]
    cumul = jnp.cumsum(logdecay, axis=-1)
    differ = cumul[..., :, None] - cumul[..., None, :]
    row_ids = lax.broadcasted_iota(jnp.int32, (size, size), 0)
    col_ids = lax.broadcasted_iota(jnp.int32, (size, size), 1)
    inclusive = col_ids <= row_ids
    strict = col_ids < row_ids
    ratio = jnp.where(inclusive, jnp.exp(jnp.where(inclusive, differ, 0.0)), 0.0)
    key_key = jnp.einsum("...te,...se->...ts", keys, keys, precision=highest)
    query_key = jnp.einsum("...te,...se->...ts", query, keys, precision=highest)
    lower = jnp.where(strict, beta[..., :, None] * ratio * key_key, 0.0) + jnp.eye(
        size, dtype=jnp.float32
    )
    rhs_values = beta[..., None] * values
    rhs_keys = (beta * jnp.exp(cumul))[..., None] * keys
    update = lax.linalg.triangular_solve(
        lower, rhs_values, left_side=True, lower=True, unit_diagonal=True
    )
    weights = lax.linalg.triangular_solve(
        lower, rhs_keys, left_side=True, lower=True, unit_diagonal=True
    )
    mixing = ratio * query_key
    decayed_query = jnp.exp(cumul)[..., None] * query
    key_end = jnp.exp(cumul[..., -1:] - cumul)[..., None] * keys
    transit = jnp.exp(cumul[..., -1])[..., None, None] * jnp.eye(width, dtype=jnp.float32)
    transit = transit - jnp.einsum("...se,...sf->...ef", key_end, weights, precision=highest)
    inject = jnp.einsum("...se,...sf->...ef", key_end, update, precision=highest)
    return (update, weights, mixing, decayed_query, transit, inject)


def run_blocks(terms, start):
    highest = lax.Precision.HIGHEST

    def advance(state, item):
        update, weights, mixing, decayed_query, transit, inject = item
        resid = update - jnp.einsum("...ce,...ef->...cf", weights, state, precision=highest)
        result = jnp.einsum("...ce,...ef->...cf", decayed_query, state, precision=highest)
        result = result + jnp.einsum("...ts,...sf->...tf", mixing, resid, precision=highest)
        state = jnp.einsum("...ef,...fg->...eg", transit, state, precision=highest) + inject
        return (state, result)

    return lax.scan(advance, start, terms)


def matmul_heads(left, right):
    return jnp.einsum("hef,hfg->heg", left, right, precision=lax.Precision.HIGHEST)


def on_device(
    query, keys, values, gate_logit, beta_logit, decay_rate, norm_gain, gate_z, out_weight
):
    tok_rows = query.shape[0]
    local_heads = values.shape[1] // DV
    key_heads = query.shape[1] // DK
    blocks = tok_rows // SPAN

    def to_blocks(array, width):
        return array.reshape(blocks, SPAN, local_heads, width).transpose(0, 2, 1, 3)

    qn = jnp.repeat(
        unit_norm(query.astype(jnp.float32).reshape(tok_rows, key_heads, DK)), 2, axis=1
    )
    kn = jnp.repeat(unit_norm(keys.astype(jnp.float32).reshape(tok_rows, key_heads, DK)), 2, axis=1)
    vals = values.astype(jnp.float32).reshape(tok_rows, local_heads, DV)
    logdecay = -decay_rate[None, :] * jax.nn.softplus(gate_logit)
    beta = jax.nn.sigmoid(beta_logit)
    terms = block_terms(
        to_blocks(qn, DK),
        to_blocks(kn, DK),
        to_blocks(vals, DV),
        logdecay.reshape(blocks, SPAN, local_heads).transpose(0, 2, 1),
        beta.reshape(blocks, SPAN, local_heads).transpose(0, 2, 1),
    )
    ident = jnp.broadcast_to(jnp.eye(DK, dtype=jnp.float32), (local_heads, DK, DK))
    zeros = jnp.zeros((local_heads, DK, DV), jnp.float32)

    def compose(carry, item):
        transit, inject = item
        return ((matmul_heads(transit, carry[0]), matmul_heads(transit, carry[1]) + inject), None)

    (shard_transit, shard_inject), unused = lax.scan(compose, (ident, zeros), (terms[4], terms[5]))

    def relay(step, carry):
        ending = matmul_heads(shard_transit, carry) + shard_inject
        return passed_along(ending, "seq", 1)

    start = lax.fori_loop(0, lax.axis_size("seq") - 1, relay, zeros)
    final, outs = run_blocks(terms, start)
    core = outs.transpose(0, 2, 1, 3).reshape(tok_rows, local_heads, DV)
    gate = jax.nn.silu(gate_z.astype(jnp.float32).reshape(tok_rows, local_heads, DV))
    scale = lax.rsqrt(jnp.mean(core * core, axis=-1, keepdims=True) + 1e-06)
    gated = (
        (core * scale * norm_gain * gate).astype(jnp.bfloat16).reshape(tok_rows, local_heads * DV)
    )
    rows = lax.all_to_all(gated, "head", split_axis=0, concat_axis=1, tiled=True)
    mixed = jnp.dot(
        rows,
        lax.all_gather(out_weight, "head", axis=0, tiled=True),
        preferred_element_type=jnp.float32,
    )
    return mixed.astype(jnp.bfloat16)


def solution(mesh):
    return jax.shard_map(
        on_device,
        mesh=mesh,
        in_specs=(
            P("seq", "head"),
            P("seq", "head"),
            P("seq", "head"),
            P("seq", "head"),
            P("seq", "head"),
            P("head"),
            P(),
            P("seq", "head"),
            P("head", None),
        ),
        out_specs=P(("seq", "head"), None),
        check_vma=False,
    )
```

profile of v0, /device:TPU:60, one launch (start us, length us, event | category | flops | bytes accessed | tf_op | source)
XLA Modules:
  0.0 640.9 jit_solution(6673752401664360787)
XLA Ops:
  12.7 2.0 fusion.30
  14.6 157.3 %custom-call.5 = f32[8,4,1,64,64]{3,4,2,1,0:T(8,128)S(1)} custom-call(f32[8,4,1,64,64]{4,3,2,1,0:T(8,128)S(1)} %fusion.30), custom_call_target="InvertDiagBlocksLowerTriangular" | custom-call | tf_op jit(solution)/shard_map/triangular_solve/custom-call.1 | solution.py:42
  178.4 2.1 fusion.36
  180.6 2.8 convolution_multiply_fusion
  183.4 4.8 fusion.44
  188.2 3.9 multiply_subtract_fusion
  192.2 14.6 %while.37 = (s32[]{:T(128)}, f32[4,128,128]{2,1,0:T(8,128)S(1)}, f32[4,128,128]{2,1,0:T(8,128)S(1)}, f32[8,4,128,128]{3,2,1,0:T(8,128)S(1)}, f32[8,4,128,128]{3,2,1,0:T(8,128)}, /*index=5*/s32[]{:T(128)}, s32[]{:T(128)}) while((s32[]{:T(128)}, f32[4,128,128]{2,1,0:T(8,128)S(1)}, f32[4,128,128]{2,1,0:T(8,128)S(1)}, ...), condition=%wide.region_3.5_spmd.clone, body=%wide.region_2.0_spmd.clone.sunk | while | flops 201457664 | bytes 2884699 | solution.py:104
  206.8 355.5 %while.35 = (s32[]{:T(128)}, f32[4,128,128]{2,1,0:T(8,128)S(1)}, f32[4,128,128]{2,1,0:T(8,128)S(1)}, f32[4,128,128]{2,1,0:T(8,128)S(1)}, s32[]{:T(128)}) while((s32[]{:T(128)}, f32[4,128,128]{2,1,0:T(8,128)S(1)}, f32[4,128,128]{2,1,0:T(8,128)S(1)}, f32[4,128,128]{2,1,0:T(8,128)S(1)}, s32[]{:T(128)}) %tuple.62), condition=%wide.region_5.7_spmd, body=%wide.region_4.6_spmd.sunk | while | flops 100728832 | bytes 2097253 | solution.py:110
  207.2 3.8 collective-permute-start
  211.1 6.1 collective-permute-done
  217.6 3.8 collective-permute-start
  221.4 8.2 %collective-permute-done = f32[4,128,128]{2,1,0:T(8,128)S(1)} collective-permute-done((f32[4,128,128]{2,1,0:T(8,128)S(1)}, f32[4,128,128]{2,1,0:T(8,128)S(1)}, u32[]{:S(2)}, u32[]{:S(2)}) %collective-permute-start) | collective-permute-done | bytes 262176 | tf_op jit(solution)/shard_map/while/body/eval_jaxpr/ppermute | solution.py:14
  232.0 8.6 %collective-permute-done = f32[4,128,128]{2,1,0:T(8,128)S(1)} collective-permute-done((f32[4,128,128]{2,1,0:T(8,128)S(1)}, f32[4,128,128]{2,1,0:T(8,128)S(1)}, u32[]{:S(2)}, u32[]{:S(2)}) %collective-permute-start) | collective-permute-done | bytes 262176 | tf_op jit(solution)/shard_map/while/body/eval_jaxpr/ppermute | solution.py:14
  242.9 8.2 %collective-permute-done = f32[4,128,128]{2,1,0:T(8,128)S(1)} collective-permute-done((f32[4,128,128]{2,1,0:T(8,128)S(1)}, f32[4,128,128]{2,1,0:T(8,128)S(1)}, u32[]{:S(2)}, u32[]{:S(2)}) %collective-permute-start) | collective-permute-done | bytes 262176 | tf_op jit(solution)/shard_map/while/body/eval_jaxpr/ppermute | solution.py:14
  253.4 8.4 %collective-permute-done = f32[4,128,128]{2,1,0:T(8,128)S(1)} collective-permute-done((f32[4,128,128]{2,1,0:T(8,128)S(1)}, f32[4,128,128]{2,1,0:T(8,128)S(1)}, u32[]{:S(2)}, u32[]{:S(2)}) %collective-permute-start) | collective-permute-done | bytes 262176 | tf_op jit(solution)/shard_map/while/body/eval_jaxpr/ppermute | solution.py:14
  264.2 8.4 %collective-permute-done = f32[4,128,128]{2,1,0:T(8,128)S(1)} collective-permute-done((f32[4,128,128]{2,1,0:T(8,128)S(1)}, f32[4,128,128]{2,1,0:T(8,128)S(1)}, u32[]{:S(2)}, u32[]{:S(2)}) %collective-permute-start) | collective-permute-done | bytes 262176 | tf_op jit(solution)/shard_map/while/body/eval_jaxpr/ppermute | solution.py:14
  275.0 8.4 %collective-permute-done = f32[4,128,128]{2,1,0:T(8,128)S(1)} collective-permute-done((f32[4,128,128]{2,1,0:T(8,128)S(1)}, f32[4,128,128]{2,1,0:T(8,128)S(1)}, u32[]{:S(2)}, u32[]{:S(2)}) %collective-permute-start) | collective-permute-done | bytes 262176 | tf_op jit(solution)/shard_map/while/body/eval_jaxpr/ppermute | solution.py:14
  285.8 9.4 %collective-permute-done = f32[4,128,128]{2,1,0:T(8,128)S(1)} collective-permute-done((f32[4,128,128]{2,1,0:T(8,128)S(1)}, f32[4,128,128]{2,1,0:T(8,128)S(1)}, u32[]{:S(2)}, u32[]{:S(2)}) %collective-permute-start) | collective-permute-done | bytes 262176 | tf_op jit(solution)/shard_map/while/body/eval_jaxpr/ppermute | solution.py:14
  297.5 10.8 %collective-permute-done = f32[4,128,128]{2,1,0:T(8,128)S(1)} collective-permute-done((f32[4,128,128]{2,1,0:T(8,128)S(1)}, f32[4,128,128]{2,1,0:T(8,128)S(1)}, u32[]{:S(2)}, u32[]{:S(2)}) %collective-permute-start) | collective-permute-done | bytes 262176 | tf_op jit(solution)/shard_map/while/body/eval_jaxpr/ppermute | solution.py:14
  310.7 11.1 %collective-permute-done = f32[4,128,128]{2,1,0:T(8,128)S(1)} collective-permute-done((f32[4,128,128]{2,1,0:T(8,128)S(1)}, f32[4,128,128]{2,1,0:T(8,128)S(1)}, u32[]{:S(2)}, u32[]{:S(2)}) %collective-permute-start) | collective-permute-done | bytes 262176 | tf_op jit(solution)/shard_map/while/body/eval_jaxpr/ppermute | solution.py:14
  324.1 9.7 %collective-permute-done = f32[4,128,128]{2,1,0:T(8,128)S(1)} collective-permute-done((f32[4,128,128]{2,1,0:T(8,128)S(1)}, f32[4,128,128]{2,1,0:T(8,128)S(1)}, u32[]{:S(2)}, u32[]{:S(2)}) %collective-permute-start) | collective-permute-done | bytes 262176 | tf_op jit(solution)/shard_map/while/body/eval_jaxpr/ppermute | solution.py:14
  336.2 8.8 %collective-permute-done = f32[4,128,128]{2,1,0:T(8,128)S(1)} collective-permute-done((f32[4,128,128]{2,1,0:T(8,128)S(1)}, f32[4,128,128]{2,1,0:T(8,128)S(1)}, u32[]{:S(2)}, u32[]{:S(2)}) %collective-permute-start) | collective-permute-done | bytes 262176 | tf_op jit(solution)/shard_map/while/body/eval_jaxpr/ppermute | solution.py:14
  347.3 8.2 %collective-permute-done = f32[4,128,128]{2,1,0:T(8,128)S(1)} collective-permute-done((f32[4,128,128]{2,1,0:T(8,128)S(1)}, f32[4,128,128]{2,1,0:T(8,128)S(1)}, u32[]{:S(2)}, u32[]{:S(2)}) %collective-permute-start) | collective-permute-done | bytes 262176 | tf_op jit(solution)/shard_map/while/body/eval_jaxpr/ppermute | solution.py:14
  357.8 8.4 %collective-permute-done = f32[4,128,128]{2,1,0:T(8,128)S(1)} collective-permute-done((f32[4,128,128]{2,1,0:T(8,128)S(1)}, f32[4,128,128]{2,1,0:T(8,128)S(1)}, u32[]{:S(2)}, u32[]{:S(2)}) %collective-permute-start) | collective-permute-done | bytes 262176 | tf_op jit(solution)/shard_map/while/body/eval_jaxpr/ppermute | solution.py:14
  368.6 8.4 %collective-permute-done = f32[4,128,128]{2,1,0:T(8,128)S(1)} collective-permute-done((f32[4,128,128]{2,1,0:T(8,128)S(1)}, f32[4,128,128]{2,1,0:T(8,128)S(1)}, u32[]{:S(2)}, u32[]{:S(2)}) %collective-permute-start) | collective-permute-done | bytes 262176 | tf_op jit(solution)/shard_map/while/body/eval_jaxpr/ppermute | solution.py:14
  379.3 8.4 %collective-permute-done = f32[4,128,128]{2,1,0:T(8,128)S(1)} collective-permute-done((f32[4,128,128]{2,1,0:T(8,128)S(1)}, f32[4,128,128]{2,1,0:T(8,128)S(1)}, u32[]{:S(2)}, u32[]{:S(2)}) %collective-permute-start) | collective-permute-done | bytes 262176 | tf_op jit(solution)/shard_map/while/body/eval_jaxpr/ppermute | solution.py:14
  390.1 9.2 %collective-permute-done = f32[4,128,128]{2,1,0:T(8,128)S(1)} collective-permute-done((f32[4,128,128]{2,1,0:T(8,128)S(1)}, f32[4,128,128]{2,1,0:T(8,128)S(1)}, u32[]{:S(2)}, u32[]{:S(2)}) %collective-permute-start) | collective-permute-done | bytes 262176 | tf_op jit(solution)/shard_map/while/body/eval_jaxpr/ppermute | solution.py:14
  401.7 10.7 %collective-permute-done = f32[4,128,128]{2,1,0:T(8,128)S(1)} collective-permute-done((f32[4,128,128]{2,1,0:T(8,128)S(1)}, f32[4,128,128]{2,1,0:T(8,128)S(1)}, u32[]{:S(2)}, u32[]{:S(2)}) %collective-permute-start) | collective-permute-done | bytes 262176 | tf_op jit(solution)/shard_map/while/body/eval_jaxpr/ppermute | solution.py:14
  414.7 11.2 %collective-permute-done = f32[4,128,128]{2,1,0:T(8,128)S(1)} collective-permute-done((f32[4,128,128]{2,1,0:T(8,128)S(1)}, f32[4,128,128]{2,1,0:T(8,128)S(1)}, u32[]{:S(2)}, u32[]{:S(2)}) %collective-permute-start) | collective-permute-done | bytes 262176 | tf_op jit(solution)/shard_map/while/body/eval_jaxpr/ppermute | solution.py:14
  428.3 9.8 %collective-permute-done = f32[4,128,128]{2,1,0:T(8,128)S(1)} collective-permute-done((f32[4,128,128]{2,1,0:T(8,128)S(1)}, f32[4,128,128]{2,1,0:T(8,128)S(1)}, u32[]{:S(2)}, u32[]{:S(2)}) %collective-permute-start) | collective-permute-done | bytes 262176 | tf_op jit(solution)/shard_map/while/body/eval_jaxpr/ppermute | solution.py:14
  440.5 8.9 %collective-permute-done = f32[4,128,128]{2,1,0:T(8,128)S(1)} collective-permute-done((f32[4,128,128]{2,1,0:T(8,128)S(1)}, f32[4,128,128]{2,1,0:T(8,128)S(1)}, u32[]{:S(2)}, u32[]{:S(2)}) %collective-permute-start) | collective-permute-done | bytes 262176 | tf_op jit(solution)/shard_map/while/body/eval_jaxpr/ppermute | solution.py:14
  451.7 8.2 %collective-permute-done = f32[4,128,128]{2,1,0:T(8,128)S(1)} collective-permute-done((f32[4,128,128]{2,1,0:T(8,128)S(1)}, f32[4,128,128]{2,1,0:T(8,128)S(1)}, u32[]{:S(2)}, u32[]{:S(2)}) %collective-permute-start) | collective-permute-done | bytes 262176 | tf_op jit(solution)/shard_map/while/body/eval_jaxpr/ppermute | solution.py:14
  462.2 8.4 %collective-permute-done = f32[4,128,128]{2,1,0:T(8,128)S(1)} collective-permute-done((f32[4,128,128]{2,1,0:T(8,128)S(1)}, f32[4,128,128]{2,1,0:T(8,128)S(1)}, u32[]{:S(2)}, u32[]{:S(2)}) %collective-permute-start) | collective-permute-done | bytes 262176 | tf_op jit(solution)/shard_map/while/body/eval_jaxpr/ppermute | solution.py:14
  473.0 8.4 %collective-permute-done = f32[4,128,128]{2,1,0:T(8,128)S(1)} collective-permute-done((f32[4,128,128]{2,1,0:T(8,128)S(1)}, f32[4,128,128]{2,1,0:T(8,128)S(1)}, u32[]{:S(2)}, u32[]{:S(2)}) %collective-permute-start) | collective-permute-done | bytes 262176 | tf_op jit(solution)/shard_map/while/body/eval_jaxpr/ppermute | solution.py:14
  483.8 8.4 %collective-permute-done = f32[4,128,128]{2,1,0:T(8,128)S(1)} collective-permute-done((f32[4,128,128]{2,1,0:T(8,128)S(1)}, f32[4,128,128]{2,1,0:T(8,128)S(1)}, u32[]{:S(2)}, u32[]{:S(2)}) %collective-permute-start) | collective-permute-done | bytes 262176 | tf_op jit(solution)/shard_map/while/body/eval_jaxpr/ppermute | solution.py:14
  494.5 9.1 %collective-permute-done = f32[4,128,128]{2,1,0:T(8,128)S(1)} collective-permute-done((f32[4,128,128]{2,1,0:T(8,128)S(1)}, f32[4,128,128]{2,1,0:T(8,128)S(1)}, u32[]{:S(2)}, u32[]{:S(2)}) %collective-permute-start) | collective-permute-done | bytes 262176 | tf_op jit(solution)/shard_map/while/body/eval_jaxpr/ppermute | solution.py:14
  506.0 10.6 %collective-permute-done = f32[4,128,128]{2,1,0:T(8,128)S(1)} collective-permute-done((f32[4,128,128]{2,1,0:T(8,128)S(1)}, f32[4,128,128]{2,1,0:T(8,128)S(1)}, u32[]{:S(2)}, u32[]{:S(2)}) %collective-permute-start) | collective-permute-done | bytes 262176 | tf_op jit(solution)/shard_map/while/body/eval_jaxpr/ppermute | solution.py:14
  518.9 11.3 %collective-permute-done = f32[4,128,128]{2,1,0:T(8,128)S(1)} collective-permute-done((f32[4,128,128]{2,1,0:T(8,128)S(1)}, f32[4,128,128]{2,1,0:T(8,128)S(1)}, u32[]{:S(2)}, u32[]{:S(2)}) %collective-permute-start) | collective-permute-done | bytes 262176 | tf_op jit(solution)/shard_map/while/body/eval_jaxpr/ppermute | solution.py:14
  532.6 8.2 %collective-permute-done = f32[4,128,128]{2,1,0:T(8,128)S(1)} collective-permute-done((f32[4,128,128]{2,1,0:T(8,128)S(1)}, f32[4,128,128]{2,1,0:T(8,128)S(1)}, u32[]{:S(2)}, u32[]{:S(2)}) %collective-permute-start) | collective-permute-done | bytes 262176 | tf_op jit(solution)/shard_map/while/body/eval_jaxpr/ppermute | solution.py:14
  543.1 8.4 %collective-permute-done = f32[4,128,128]{2,1,0:T(8,128)S(1)} collective-permute-done((f32[4,128,128]{2,1,0:T(8,128)S(1)}, f32[4,128,128]{2,1,0:T(8,128)S(1)}, u32[]{:S(2)}, u32[]{:S(2)}) %collective-permute-start) | collective-permute-done | bytes 262176 | tf_op jit(solution)/shard_map/while/body/eval_jaxpr/ppermute | solution.py:14
  553.9 8.4 %collective-permute-done = f32[4,128,128]{2,1,0:T(8,128)S(1)} collective-permute-done((f32[4,128,128]{2,1,0:T(8,128)S(1)}, f32[4,128,128]{2,1,0:T(8,128)S(1)}, u32[]{:S(2)}, u32[]{:S(2)}) %collective-permute-start) | collective-permute-done | bytes 262176 | tf_op jit(solution)/shard_map/while/body/eval_jaxpr/ppermute | solution.py:14
  562.3 46.7 %while.36 = (s32[]{:T(128)}, f32[4,128,128]{2,1,0:T(8,128)S(1)}, f32[8,4,64,128]{3,2,1,0:T(8,128)}, f32[8,4,128,128]{3,2,1,0:T(8,128)S(1)}, f32[8,4,128,128]{3,2...) while((s32[]{:T(128)}, f32[4,128,128]{2,1,0:T(8,128)S(1)}, ...), condition=%wide.region_8.10_spmd, body=%wide.region_7.9_spmd.sunk | while | flops 226623488 | bytes 3280485 | solution.py:65
  564.9 1.9 fusion.96
  582.4 1.9 fusion.96
  599.9 1.9 fusion.96
  605.8 1.9 fusion.96
  612.7 11.8 %all_to_all.19 = bf16[8,64,512]{2,1,0:T(8,128)(2,1)S(1)} all-to-all(bf16[8,64,512]{2,1,0:T(8,128)(2,1)S(1)} %bitcast.135), channel_id=1, replica_groups=mesh['seq'=32,'head'=8] {'head'}, dimensions={0} | all-to-all | bytes 1048576 | tf_op jit(solution)/shard_map/all_to_all | solution.py:118
  624.6 9.5 %convolution_convert_fusion = bf16[64,2048]{1,0:T(8,128)(2,1)} fusion(bf16[64,4096]{1,0:T(8,128)(2,1)S(1)} %bitcast.133, bf16[4096,2048]{1,0:T(8,128)(2,1)} %all-gather.2.cloned.1.call-done), kind=kOutput, calls=%fused_computation.31 | convolution fusion | flops 1073872896 | bytes 17563648 | tf_op jit(solution)/shard_map/dot_general | solution.py:119
  (195 shorter events, 136.9 us)
Async XLA Ops:
  6.5 605.1 %copy-start = (f32[128]{0:T(128)S(1)}, f32[128]{0:T(128)}, u32[]{:S(2)}) copy-start(f32[128]{0:T(128)} %param.23) | copy-start | bytes 1540
  6.5 0.8 copy-start.9
  6.5 0.8 copy-start.7
  6.5 0.9 copy-start.8
  6.5 1.0 copy-start.5
  6.5 618.0 %all-gather.2.cloned.1.call-start = ((), (), s32[]{:S(2)}) async-start(), calls=%async_computation.1 | async-start | bytes 18874368 | tf_op jit(solution)/shard_map/all_gather | solution.py:121
  7.6 1.6 copy-start.6
  178.4 9.8 %copy-start.1 = (f32[8,4,64,128]{3,2,1,0:T(8,128)}, f32[8,4,64,128]{3,2,1,0:T(8,128)S(1)}, u32[]{:S(2)}) copy-start(f32[8,4,64,128]{3,2,1,0:T(8,128)S(1)} %fusion.38) | copy-start | bytes 3145732
  180.6 7.7 %copy-start.2 = (f32[8,4,64,128]{3,2,1,0:T(8,128)}, f32[8,4,64,128]{3,2,1,0:T(8,128)S(1)}, u32[]{:S(2)}) copy-start(f32[8,4,64,128]{3,2,1,0:T(8,128)S(1)} %fusion.36) | copy-start | bytes 3145732
  207.2 9.9 %collective-permute-start = (f32[4,128,128]{2,1,0:T(8,128)S(1)}, f32[4,128,128]{2,1,0:T(8,128)S(1)}, u32[]{:S(2)}, u32[]{:S(2)}) collective-permute-start(f32[4,128,128]{2,1,0:T(8,128)S(1)} %convolution_add_fusion.7), channel_id=1, source_target_pairs={{0,8},{8,16},{16,24},{24,32},{32,40},{40,48},{48,56},{56,64},{64,7... | collective-permute-start | bytes 786440 | tf_op jit(solution)/shard_map/while/body/eval_jaxpr/ppermute | solution.py:14
  217.6 12.1 %collective-permute-start = (f32[4,128,128]{2,1,0:T(8,128)S(1)}, f32[4,128,128]{2,1,0:T(8,128)S(1)}, u32[]{:S(2)}, u32[]{:S(2)}) collective-permute-start(f32[4,128,128]{2,1,0:T(8,128)S(1)} %convolution_add_fusion.7), channel_id=1, source_target_pairs={{0,8},{8,16},{16,24},{24,32},{32,40},{40,48},{48,56},{56,64},{64,7... | collective-permute-start | bytes 786440 | tf_op jit(solution)/shard_map/while/body/eval_jaxpr/ppermute | solution.py:14
  230.0 10.6 %collective-permute-start = (f32[4,128,128]{2,1,0:T(8,128)S(1)}, f32[4,128,128]{2,1,0:T(8,128)S(1)}, u32[]{:S(2)}, u32[]{:S(2)}) collective-permute-start(f32[4,128,128]{2,1,0:T(8,128)S(1)} %convolution_add_fusion.7), channel_id=1, source_target_pairs={{0,8},{8,16},{16,24},{24,32},{32,40},{40,48},{48,56},{56,64},{64,7... | collective-permute-start | bytes 786440 | tf_op jit(solution)/shard_map/while/body/eval_jaxpr/ppermute | solution.py:14
  241.0 10.1 %collective-permute-start = (f32[4,128,128]{2,1,0:T(8,128)S(1)}, f32[4,128,128]{2,1,0:T(8,128)S(1)}, u32[]{:S(2)}, u32[]{:S(2)}) collective-permute-start(f32[4,128,128]{2,1,0:T(8,128)S(1)} %convolution_add_fusion.7), channel_id=1, source_target_pairs={{0,8},{8,16},{16,24},{24,32},{32,40},{40,48},{48,56},{56,64},{64,7... | collective-permute-start | bytes 786440 | tf_op jit(solution)/shard_map/while/body/eval_jaxpr/ppermute | solution.py:14
  251.5 10.4 %collective-permute-start = (f32[4,128,128]{2,1,0:T(8,128)S(1)}, f32[4,128,128]{2,1,0:T(8,128)S(1)}, u32[]{:S(2)}, u32[]{:S(2)}) collective-permute-start(f32[4,128,128]{2,1,0:T(8,128)S(1)} %convolution_add_fusion.7), channel_id=1, source_target_pairs={{0,8},{8,16},{16,24},{24,32},{32,40},{40,48},{48,56},{56,64},{64,7... | collective-permute-start | bytes 786440 | tf_op jit(solution)/shard_map/while/body/eval_jaxpr/ppermute | solution.py:14
  262.3 10.4 %collective-permute-start = (f32[4,128,128]{2,1,0:T(8,128)S(1)}, f32[4,128,128]{2,1,0:T(8,128)S(1)}, u32[]{:S(2)}, u32[]{:S(2)}) collective-permute-start(f32[4,128,128]{2,1,0:T(8,128)S(1)} %convolution_add_fusion.7), channel_id=1, source_target_pairs={{0,8},{8,16},{16,24},{24,32},{32,40},{40,48},{48,56},{56,64},{64,7... | collective-permute-start | bytes 786440 | tf_op jit(solution)/shard_map/while/body/eval_jaxpr/ppermute | solution.py:14
  273.1 10.4 %collective-permute-start = (f32[4,128,128]{2,1,0:T(8,128)S(1)}, f32[4,128,128]{2,1,0:T(8,128)S(1)}, u32[]{:S(2)}, u32[]{:S(2)}) collective-permute-start(f32[4,128,128]{2,1,0:T(8,128)S(1)} %convolution_add_fusion.7), channel_id=1, source_target_pairs={{0,8},{8,16},{16,24},{24,32},{32,40},{40,48},{48,56},{56,64},{64,7... | collective-permute-start | bytes 786440 | tf_op jit(solution)/shard_map/while/body/eval_jaxpr/ppermute | solution.py:14
  283.8 11.4 %collective-permute-start = (f32[4,128,128]{2,1,0:T(8,128)S(1)}, f32[4,128,128]{2,1,0:T(8,128)S(1)}, u32[]{:S(2)}, u32[]{:S(2)}) collective-permute-start(f32[4,128,128]{2,1,0:T(8,128)S(1)} %convolution_add_fusion.7), channel_id=1, source_target_pairs={{0,8},{8,16},{16,24},{24,32},{32,40},{40,48},{48,56},{56,64},{64,7... | collective-permute-start | bytes 786440 | tf_op jit(solution)/shard_map/while/body/eval_jaxpr/ppermute | solution.py:14
  295.6 12.7 %collective-permute-start = (f32[4,128,128]{2,1,0:T(8,128)S(1)}, f32[4,128,128]{2,1,0:T(8,128)S(1)}, u32[]{:S(2)}, u32[]{:S(2)}) collective-permute-start(f32[4,128,128]{2,1,0:T(8,128)S(1)} %convolution_add_fusion.7), channel_id=1, source_target_pairs={{0,8},{8,16},{16,24},{24,32},{32,40},{40,48},{48,56},{56,64},{64,7... | collective-permute-start | bytes 786440 | tf_op jit(solution)/shard_map/while/body/eval_jaxpr/ppermute | solution.py:14
  308.8 13.1 %collective-permute-start = (f32[4,128,128]{2,1,0:T(8,128)S(1)}, f32[4,128,128]{2,1,0:T(8,128)S(1)}, u32[]{:S(2)}, u32[]{:S(2)}) collective-permute-start(f32[4,128,128]{2,1,0:T(8,128)S(1)} %convolution_add_fusion.7), channel_id=1, source_target_pairs={{0,8},{8,16},{16,24},{24,32},{32,40},{40,48},{48,56},{56,64},{64,7... | collective-permute-start | bytes 786440 | tf_op jit(solution)/shard_map/while/body/eval_jaxpr/ppermute | solution.py:14
  322.2 11.6 %collective-permute-start = (f32[4,128,128]{2,1,0:T(8,128)S(1)}, f32[4,128,128]{2,1,0:T(8,128)S(1)}, u32[]{:S(2)}, u32[]{:S(2)}) collective-permute-start(f32[4,128,128]{2,1,0:T(8,128)S(1)} %convolution_add_fusion.7), channel_id=1, source_target_pairs={{0,8},{8,16},{16,24},{24,32},{32,40},{40,48},{48,56},{56,64},{64,7... | collective-permute-start | bytes 786440 | tf_op jit(solution)/shard_map/while/body/eval_jaxpr/ppermute | solution.py:14
  334.2 10.7 %collective-permute-start = (f32[4,128,128]{2,1,0:T(8,128)S(1)}, f32[4,128,128]{2,1,0:T(8,128)S(1)}, u32[]{:S(2)}, u32[]{:S(2)}) collective-permute-start(f32[4,128,128]{2,1,0:T(8,128)S(1)} %convolution_add_fusion.7), channel_id=1, source_target_pairs={{0,8},{8,16},{16,24},{24,32},{32,40},{40,48},{48,56},{56,64},{64,7... | collective-permute-start | bytes 786440 | tf_op jit(solution)/shard_map/while/body/eval_jaxpr/ppermute | solution.py:14
  345.4 10.1 %collective-permute-start = (f32[4,128,128]{2,1,0:T(8,128)S(1)}, f32[4,128,128]{2,1,0:T(8,128)S(1)}, u32[]{:S(2)}, u32[]{:S(2)}) collective-permute-start(f32[4,128,128]{2,1,0:T(8,128)S(1)} %convolution_add_fusion.7), channel_id=1, source_target_pairs={{0,8},{8,16},{16,24},{24,32},{32,40},{40,48},{48,56},{56,64},{64,7... | collective-permute-start | bytes 786440 | tf_op jit(solution)/shard_map/while/body/eval_jaxpr/ppermute | solution.py:14
  355.9 10.4 %collective-permute-start = (f32[4,128,128]{2,1,0:T(8,128)S(1)}, f32[4,128,128]{2,1,0:T(8,128)S(1)}, u32[]{:S(2)}, u32[]{:S(2)}) collective-permute-start(f32[4,128,128]{2,1,0:T(8,128)S(1)} %convolution_add_fusion.7), channel_id=1, source_target_pairs={{0,8},{8,16},{16,24},{24,32},{32,40},{40,48},{48,56},{56,64},{64,7... | collective-permute-start | bytes 786440 | tf_op jit(solution)/shard_map/while/body/eval_jaxpr/ppermute | solution.py:14
  366.6 10.4 %collective-permute-start = (f32[4,128,128]{2,1,0:T(8,128)S(1)}, f32[4,128,128]{2,1,0:T(8,128)S(1)}, u32[]{:S(2)}, u32[]{:S(2)}) collective-permute-start(f32[4,128,128]{2,1,0:T(8,128)S(1)} %convolution_add_fusion.7), channel_id=1, source_target_pairs={{0,8},{8,16},{16,24},{24,32},{32,40},{40,48},{48,56},{56,64},{64,7... | collective-permute-start | bytes 786440 | tf_op jit(solution)/shard_map/while/body/eval_jaxpr/ppermute | solution.py:14
  377.4 10.4 %collective-permute-start = (f32[4,128,128]{2,1,0:T(8,128)S(1)}, f32[4,128,128]{2,1,0:T(8,128)S(1)}, u32[]{:S(2)}, u32[]{:S(2)}) collective-permute-start(f32[4,128,128]{2,1,0:T(8,128)S(1)} %convolution_add_fusion.7), channel_id=1, source_target_pairs={{0,8},{8,16},{16,24},{24,32},{32,40},{40,48},{48,56},{56,64},{64,7... | collective-permute-start | bytes 786440 | tf_op jit(solution)/shard_map/while/body/eval_jaxpr/ppermute | solution.py:14
  388.2 11.2 %collective-permute-start = (f32[4,128,128]{2,1,0:T(8,128)S(1)}, f32[4,128,128]{2,1,0:T(8,128)S(1)}, u32[]{:S(2)}, u32[]{:S(2)}) collective-permute-start(f32[4,128,128]{2,1,0:T(8,128)S(1)} %convolution_add_fusion.7), channel_id=1, source_target_pairs={{0,8},{8,16},{16,24},{24,32},{32,40},{40,48},{48,56},{56,64},{64,7... | collective-permute-start | bytes 786440 | tf_op jit(solution)/shard_map/while/body/eval_jaxpr/ppermute | solution.py:14
  399.8 12.6 %collective-permute-start = (f32[4,128,128]{2,1,0:T(8,128)S(1)}, f32[4,128,128]{2,1,0:T(8,128)S(1)}, u32[]{:S(2)}, u32[]{:S(2)}) collective-permute-start(f32[4,128,128]{2,1,0:T(8,128)S(1)} %convolution_add_fusion.7), channel_id=1, source_target_pairs={{0,8},{8,16},{16,24},{24,32},{32,40},{40,48},{48,56},{56,64},{64,7... | collective-permute-start | bytes 786440 | tf_op jit(solution)/shard_map/while/body/eval_jaxpr/ppermute | solution.py:14
  412.8 13.2 %collective-permute-start = (f32[4,128,128]{2,1,0:T(8,128)S(1)}, f32[4,128,128]{2,1,0:T(8,128)S(1)}, u32[]{:S(2)}, u32[]{:S(2)}) collective-permute-start(f32[4,128,128]{2,1,0:T(8,128)S(1)} %convolution_add_fusion.7), channel_id=1, source_target_pairs={{0,8},{8,16},{16,24},{24,32},{32,40},{40,48},{48,56},{56,64},{64,7... | collective-permute-start | bytes 786440 | tf_op jit(solution)/shard_map/while/body/eval_jaxpr/ppermute | solution.py:14
  426.4 11.8 %collective-permute-start = (f32[4,128,128]{2,1,0:T(8,128)S(1)}, f32[4,128,128]{2,1,0:T(8,128)S(1)}, u32[]{:S(2)}, u32[]{:S(2)}) collective-permute-start(f32[4,128,128]{2,1,0:T(8,128)S(1)} %convolution_add_fusion.7), channel_id=1, source_target_pairs={{0,8},{8,16},{16,24},{24,32},{32,40},{40,48},{48,56},{56,64},{64,7... | collective-permute-start | bytes 786440 | tf_op jit(solution)/shard_map/while/body/eval_jaxpr/ppermute | solution.py:14
  438.5 10.8 %collective-permute-start = (f32[4,128,128]{2,1,0:T(8,128)S(1)}, f32[4,128,128]{2,1,0:T(8,128)S(1)}, u32[]{:S(2)}, u32[]{:S(2)}) collective-permute-start(f32[4,128,128]{2,1,0:T(8,128)S(1)} %convolution_add_fusion.7), channel_id=1, source_target_pairs={{0,8},{8,16},{16,24},{24,32},{32,40},{40,48},{48,56},{56,64},{64,7... | collective-permute-start | bytes 786440 | tf_op jit(solution)/shard_map/while/body/eval_jaxpr/ppermute | solution.py:14
  449.8 10.1 %collective-permute-start = (f32[4,128,128]{2,1,0:T(8,128)S(1)}, f32[4,128,128]{2,1,0:T(8,128)S(1)}, u32[]{:S(2)}, u32[]{:S(2)}) collective-permute-start(f32[4,128,128]{2,1,0:T(8,128)S(1)} %convolution_add_fusion.7), channel_id=1, source_target_pairs={{0,8},{8,16},{16,24},{24,32},{32,40},{40,48},{48,56},{56,64},{64,7... | collective-permute-start | bytes 786440 | tf_op jit(solution)/shard_map/while/body/eval_jaxpr/ppermute | solution.py:14
  460.3 10.4 %collective-permute-start = (f32[4,128,128]{2,1,0:T(8,128)S(1)}, f32[4,128,128]{2,1,0:T(8,128)S(1)}, u32[]{:S(2)}, u32[]{:S(2)}) collective-permute-start(f32[4,128,128]{2,1,0:T(8,128)S(1)} %convolution_add_fusion.7), channel_id=1, source_target_pairs={{0,8},{8,16},{16,24},{24,32},{32,40},{40,48},{48,56},{56,64},{64,7... | collective-permute-start | bytes 786440 | tf_op jit(solution)/shard_map/while/body/eval_jaxpr/ppermute | solution.py:14
  471.1 10.4 %collective-permute-start = (f32[4,128,128]{2,1,0:T(8,128)S(1)}, f32[4,128,128]{2,1,0:T(8,128)S(1)}, u32[]{:S(2)}, u32[]{:S(2)}) collective-permute-start(f32[4,128,128]{2,1,0:T(8,128)S(1)} %convolution_add_fusion.7), channel_id=1, source_target_pairs={{0,8},{8,16},{16,24},{24,32},{32,40},{40,48},{48,56},{56,64},{64,7... | collective-permute-start | bytes 786440 | tf_op jit(solution)/shard_map/while/body/eval_jaxpr/ppermute | solution.py:14
  481.8 10.4 %collective-permute-start = (f32[4,128,128]{2,1,0:T(8,128)S(1)}, f32[4,128,128]{2,1,0:T(8,128)S(1)}, u32[]{:S(2)}, u32[]{:S(2)}) collective-permute-start(f32[4,128,128]{2,1,0:T(8,128)S(1)} %convolution_add_fusion.7), channel_id=1, source_target_pairs={{0,8},{8,16},{16,24},{24,32},{32,40},{40,48},{48,56},{56,64},{64,7... | collective-permute-start | bytes 786440 | tf_op jit(solution)/shard_map/while/body/eval_jaxpr/ppermute | solution.py:14
  492.6 11.1 %collective-permute-start = (f32[4,128,128]{2,1,0:T(8,128)S(1)}, f32[4,128,128]{2,1,0:T(8,128)S(1)}, u32[]{:S(2)}, u32[]{:S(2)}) collective-permute-start(f32[4,128,128]{2,1,0:T(8,128)S(1)} %convolution_add_fusion.7), channel_id=1, source_target_pairs={{0,8},{8,16},{16,24},{24,32},{32,40},{40,48},{48,56},{56,64},{64,7... | collective-permute-start | bytes 786440 | tf_op jit(solution)/shard_map/while/body/eval_jaxpr/ppermute | solution.py:14
  504.1 12.5 %collective-permute-start = (f32[4,128,128]{2,1,0:T(8,128)S(1)}, f32[4,128,128]{2,1,0:T(8,128)S(1)}, u32[]{:S(2)}, u32[]{:S(2)}) collective-permute-start(f32[4,128,128]{2,1,0:T(8,128)S(1)} %convolution_add_fusion.7), channel_id=1, source_target_pairs={{0,8},{8,16},{16,24},{24,32},{32,40},{40,48},{48,56},{56,64},{64,7... | collective-permute-start | bytes 786440 | tf_op jit(solution)/shard_map/while/body/eval_jaxpr/ppermute | solution.py:14
  517.0 13.3 %collective-permute-start = (f32[4,128,128]{2,1,0:T(8,128)S(1)}, f32[4,128,128]{2,1,0:T(8,128)S(1)}, u32[]{:S(2)}, u32[]{:S(2)}) collective-permute-start(f32[4,128,128]{2,1,0:T(8,128)S(1)} %convolution_add_fusion.7), channel_id=1, source_target_pairs={{0,8},{8,16},{16,24},{24,32},{32,40},{40,48},{48,56},{56,64},{64,7... | collective-permute-start | bytes 786440 | tf_op jit(solution)/shard_map/while/body/eval_jaxpr/ppermute | solution.py:14
  530.7 10.1 %collective-permute-start = (f32[4,128,128]{2,1,0:T(8,128)S(1)}, f32[4,128,128]{2,1,0:T(8,128)S(1)}, u32[]{:S(2)}, u32[]{:S(2)}) collective-permute-start(f32[4,128,128]{2,1,0:T(8,128)S(1)} %convolution_add_fusion.7), channel_id=1, source_target_pairs={{0,8},{8,16},{16,24},{24,32},{32,40},{40,48},{48,56},{56,64},{64,7... | collective-permute-start | bytes 786440 | tf_op jit(solution)/shard_map/while/body/eval_jaxpr/ppermute | solution.py:14
  541.2 10.4 %collective-permute-start = (f32[4,128,128]{2,1,0:T(8,128)S(1)}, f32[4,128,128]{2,1,0:T(8,128)S(1)}, u32[]{:S(2)}, u32[]{:S(2)}) collective-permute-start(f32[4,128,128]{2,1,0:T(8,128)S(1)} %convolution_add_fusion.7), channel_id=1, source_target_pairs={{0,8},{8,16},{16,24},{24,32},{32,40},{40,48},{48,56},{56,64},{64,7... | collective-permute-start | bytes 786440 | tf_op jit(solution)/shard_map/while/body/eval_jaxpr/ppermute | solution.py:14
  552.0 10.4 %collective-permute-start = (f32[4,128,128]{2,1,0:T(8,128)S(1)}, f32[4,128,128]{2,1,0:T(8,128)S(1)}, u32[]{:S(2)}, u32[]{:S(2)}) collective-permute-start(f32[4,128,128]{2,1,0:T(8,128)S(1)} %convolution_add_fusion.7), channel_id=1, source_target_pairs={{0,8},{8,16},{16,24},{24,32},{32,40},{40,48},{48,56},{56,64},{64,7... | collective-permute-start | bytes 786440 | tf_op jit(solution)/shard_map/while/body/eval_jaxpr/ppermute | solution.py:14
  609.1 1.9 copy-start.3
  610.8 1.5 copy-start.4
Sparse Core Ops, SparseCore 0:
  9.2 89.6 all-gather.1
where the time goes:
time: 650 us; the launch traced here: 641 us
  waiting for transfers between devices  280 us (43%)
  other arithmetic  165 us (25%)
  matrix products  99.5 us (15%)
  starting transfers between devices  63.4 us (10%)
  between operations  13.7 us (2%)
  blocking collectives  11.8 us (2%)
    ppermute x31, waiting for transfers between devices, passed_along(): return lax.ppermute(shard, axis, pairs)  279 us
    another operation x4, other arithmetic, block_terms(): lax.linalg.triangular_solve(lower, rhs_keys, left_side=True, lower=True,...  157 us
    ppermute x31, starting transfers between devices, passed_along(): return lax.ppermute(shard, axis, pairs)  63.3 us
    dot_general x47, matrix products, matmul_heads(): jnp.einsum('hef,hfg->heg', left, right, precision=lax.Precision.HIGHEST)  26.2 us
    dot_general x8, matrix products, advance(): jnp.einsum('...ce,...ef->...cf', decayed_query, state, precision=highest)  15.5 us
  transfers between devices with their start and end apart: 32, of which 31 were waited for; matrix products, arithmetic and copies ran while one was open for 41% of the time, Pallas kernels for 0%

commit v1 on v0

v1 whole, which is shorter than its diff:
```python
import jax
import jax.numpy as jnp
from jax import lax
from jax.experimental import pallas as pl
from jax.experimental.pallas import tpu as pltpu
from jax.sharding import PartitionSpec as P

BLK = 128
NB = 4
NH = 4
NY = 4
NZ = 8
NX = 4
ROWS_D = 128
ROWS_C = 144
ROWS_M = 272
F32 = jnp.float32
BF16 = jnp.bfloat16


def dot(left, right):
    return jnp.dot(left, right, preferred_element_type=F32)


def dot_nt(left, right):
    return lax.dot_general(left, right, (((1,), (1,)), ((), ())), preferred_element_type=F32)


def split3(x):
    hi = x.astype(BF16)
    rest = x - hi.astype(F32)
    mid = rest.astype(BF16)
    low = (rest - mid.astype(F32)).astype(BF16)
    return hi, mid, low


def softplus(x):
    y = jnp.exp(-jnp.abs(x))
    small = y * (1.0 - y * (0.5 - y * (1.0 / 3.0 - y * 0.25)))
    return jnp.maximum(x, 0.0) + jnp.where(y < 0.01, small, jnp.log(1.0 + y))


def sigmoid(x):
    return 1.0 / (1.0 + jnp.exp(-x))


def gates(gl_ref, bl_ref, rate_ref, k_ref, q_ref, s):
    g4 = -rate_ref[...] * softplus(gl_ref[...])
    beta4 = sigmoid(bl_ref[...])
    for b in range(NB):
        s["g16"][pl.ds(4 * b, 4), :] = g4[:, BLK * b : BLK * (b + 1)]
    row_ids = lax.broadcasted_iota(jnp.int32, (BLK, BLK), 0)
    col_ids = lax.broadcasted_iota(jnp.int32, (BLK, BLK), 1)
    upper = jnp.where(row_ids <= col_ids, 1.0, 0.0).astype(BF16)
    hi, mid, low = split3(s["g16"][...])
    s["g16"][...] = dot(hi, upper) + dot(mid, upper) + dot(low, upper)
    for b in range(NB):
        for kh in range(2):
            kf = k_ref[pl.ds(BLK * b, BLK), BLK * kh : BLK * (kh + 1)].astype(F32)
            kt = kf.T
            s["kt"][2 * b + kh] = kt.astype(BF16)
            rk = lax.rsqrt(jnp.sum(kt * kt, axis=0, keepdims=True) + 1e-06)
            s["rows"][b, pl.ds(24 + 2 * kh, 1), :] = rk
            s["rows"][b, pl.ds(25 + 2 * kh, 1), :] = rk
            qf = q_ref[pl.ds(BLK * b, BLK), BLK * kh : BLK * (kh + 1)].astype(F32)
            s["rq"][kh, pl.ds(BLK * b, BLK), :] = lax.rsqrt(
                jnp.sum(qf * qf, axis=1, keepdims=True) + 1e-06
            )
        c = s["g16"][pl.ds(4 * b, 4), :]
        beta = beta4[:, BLK * b : BLK * (b + 1)]
        rk4 = s["rows"][b, pl.ds(24, 4), :]
        end = c[:, BLK - 1 : BLK]
        ec = jnp.exp(c)
        s["rows"][b, pl.ds(0, 4), :] = c
        s["rows"][b, pl.ds(4, 4), :] = beta * rk4
        s["rows"][b, pl.ds(8, 4), :] = rk4 * jnp.exp(end - c)
        s["rows"][b, pl.ds(12, 4), :] = ec
        s["rows"][b, pl.ds(16, 4), :] = beta
        s["rows"][b, pl.ds(20, 4), :] = beta * rk4 * ec
        s["rows"][b, pl.ds(28, 4), :] = jnp.exp(jnp.broadcast_to(end, (4, BLK)))
        s["cols"][b] = s["rows"][b].T


def block_terms(k_ref, q_ref, v_ref, s):
    row_ids = lax.broadcasted_iota(jnp.int32, (BLK, BLK), 0)
    col_ids = lax.broadcasted_iota(jnp.int32, (BLK, BLK), 1)
    inclusive = col_ids <= row_ids
    differ = row_ids ^ col_ids
    ident = jnp.where(row_ids == col_ids, 1.0, 0.0)

    def group(g, carry):
        lower = {}
        for i in range(2):
            b = 2 * g + i
            tok = pl.ds(pl.multiple_of(b * BLK, BLK), BLK)
            cols = s["cols"][b]
            for kh in range(2):
                kt = s["kt"][2 * b + kh]
                kk = dot(k_ref[tok, BLK * kh : BLK * (kh + 1)], kt)
                qk = dot(q_ref[tok, BLK * kh : BLK * (kh + 1)], kt)
                rk = s["rows"][b, pl.ds(24 + 2 * kh, 1), :]
                for h in (2 * kh, 2 * kh + 1):
                    gap = cols[:, h : h + 1] - s["rows"][b, pl.ds(h, 1), :]
                    ratio = jnp.exp(jnp.where(inclusive, gap, -1e30)) * rk
                    s["mix"][4 * b + h] = (ratio * qk).astype(BF16)
                    lower[i, h] = cols[:, 4 + h : 5 + h] * ratio * kk
                    s["low"][4 * i + h] = lower[i, h]
        pairs = [(i, h) for i in range(2) for h in range(NH)]
        for p in pairs:
            off = jnp.where(differ == 1, s["low"][4 * p[0] + p[1]], 0.0)
            s["inv"][4 * p[0] + p[1]] = ident - off
        for level in range(1, 7):
            here = (differ >> level) == 1
            part = {}
            for p in pairs:
                n = 4 * p[0] + p[1]
                off = jnp.where(here, s["low"][n], 0.0).astype(BF16)
                part[p] = dot(off, s["inv"][n].astype(BF16)).astype(BF16)
            for p in pairs:
                n = 4 * p[0] + p[1]
                inv = s["inv"][n]
                s["inv"][n] = inv - dot(inv.astype(BF16), part[p])
        for i, h in pairs:
            b = 2 * g + i
            tok = pl.ds(pl.multiple_of(b * BLK, BLK), BLK)
            inv = s["inv"][4 * i + h]
            t_v = (inv * s["rows"][b, pl.ds(16 + h, 1), :]).astype(BF16)
            t_k = (inv * s["rows"][b, pl.ds(20 + h, 1), :]).astype(BF16)
            kh = h // 2
            s["upd"][4 * b + h] = dot(t_v, v_ref[tok, BLK * h : BLK * (h + 1)])
            s["wts"][4 * b + h] = dot(t_k, k_ref[tok, BLK * kh : BLK * (kh + 1)]).astype(BF16)
        return carry

    lax.fori_loop(0, NB // 2, group, 0)


def run_shard(s):
    row_ids = lax.broadcasted_iota(jnp.int32, (BLK, BLK), 0)
    col_ids = lax.broadcasted_iota(jnp.int32, (BLK, BLK), 1)
    eye = row_ids == col_ids
    for h in range(NH):
        s["state"][h, :, :BLK] = jnp.zeros((BLK, BLK), F32)
        s["state"][h, :, BLK:] = jnp.where(eye, 1.0, 0.0)

    def block(b, carry):
        cols = s["cols"][b]
        for h in range(NH):
            n = 4 * b + h
            state = s["state"][h].astype(BF16)
            s["sb"][n] = state
            ws = dot(s["wts"][n], state)
            res_s = s["upd"][n] - ws[:, :BLK]
            res_a = -ws[:, BLK:]
            end = cols[:, 8 + h : 9 + h]
            s["rb"][n, :, :BLK] = res_s.astype(BF16)
            s["rb"][n, :, BLK:] = res_a.astype(BF16)
            s["re"][h, :, :BLK] = (end * res_s).astype(BF16)
            s["re"][h, :, BLK:] = (end * res_a).astype(BF16)
        for h in range(NH):
            gain = s["rows"][b, pl.ds(28 + h, 1), :]
            grow = dot(s["kt"][2 * b + h // 2], s["re"][h])
            s["state"][h, :, :BLK] = gain * s["state"][h, :, :BLK] + grow[:, :BLK]
            s["state"][h, :, BLK:] = gain * s["state"][h, :, BLK:] + grow[:, BLK:]
        return carry

    lax.fori_loop(0, NB, block, 0)
    c_ids = lax.broadcasted_iota(jnp.int32, (16, BLK), 0)
    for h in range(NH):
        total = s["g16"][pl.ds(h, 1), :]
        for b in range(1, NB):
            total = total + s["g16"][pl.ds(4 * b + h, 1), :]
        c = jnp.exp(jnp.broadcast_to(total[:, BLK - 1 : BLK], (16, BLK)))
        hi, mid, low = (part.astype(F32) for part in split3(c))
        terms = jnp.where(c_ids == 0, hi, jnp.where(c_ids == 1, mid, jnp.where(c_ids == 2, low, 0.0)))
        fix = jnp.where(eye, c[:1], 0.0) - s["state"][h, :, BLK:]
        s["msg"][h, :ROWS_D, :] = fix.T.astype(BF16)
        s["msg"][h, ROWS_D:ROWS_C, :] = terms.astype(BF16)
        s["msg"][h, ROWS_C:, :] = s["state"][h, :, :BLK].T.astype(BF16)


def block_output(b, q_ref, s):
    tok = pl.ds(b * BLK, BLK)
    for h in range(NH):
        n = 4 * b + h
        kh = h // 2
        qs = dot(q_ref[tok, BLK * kh : BLK * (kh + 1)], s["sb"][n])
        out = s["cols"][b, :, 12 + h : 13 + h] * qs + dot(s["mix"][n], s["rb"][n])
        s["oloc"][h, tok, :] = out[:, :BLK]
        s["corr"][h, tok, :] = out[:, BLK:].astype(BF16)


def kernel(
    q_ref, k_ref, v_ref, gl_ref, bl_ref, rate_ref, gain_ref, z_hbm, w_hbm, out_ref,
    g16, rows, cols, rq, kt, mix, low, inv, upd, wts, state, sb, rb, re, msg, oloc, corr,
    z_buf, w_buf, gate, dball, bst, xst, xr, xin, gated, parta, recva, partb, sumb, recvb,
    load_sem, y_send, y_recv, rr_send, rr_recv, rl_send, rl_recv, b_send, b_recv,
    u_send, u_recv, x_send, x_recv, a_send, a_recv, e_send, e_recv,
):
    s = dict(
        g16=g16, rows=rows, cols=cols, rq=rq, kt=kt, mix=mix, low=low, inv=inv, upd=upd, wts=wts,
        state=state, sb=sb, rb=rb, re=re, msg=msg, oloc=oloc, corr=corr,
    )
    seq = lax.axis_index("seq")
    head = lax.axis_index("head")
    y, z = seq // NZ, seq % NZ
    x, core = head // 2, head % 2

    def at(y_to, z_to):
        return (y_to * NZ + z_to, head)

    def on_line(x_to, core_to):
        return (seq, 2 * x_to + core_to)

    def remote(src, dst, send, recv, device):
        return pltpu.make_async_remote_copy(
            src_ref=src, dst_ref=dst, send_sem=send, recv_sem=recv,
            device_id=device, device_id_type=pl.DeviceIdType.MESH,
        )

    peers = [at((y + i) % NY, z) for i in range(1, NY)]
    peers += [at(y, (z + i) % NZ) for i in range(1, NZ)]
    peers += [on_line((x + i) % NX, core) for i in range(1, NX)]
    peers += [on_line(x, 1 - core)]
    barrier = pltpu.get_barrier_semaphore()
    for peer in peers:
        pl.semaphore_signal(barrier, inc=1, device_id=peer, device_id_type=pl.DeviceIdType.MESH)
    load_z = pltpu.make_async_copy(z_hbm, z_buf, load_sem.at[0])
    load_w = pltpu.make_async_copy(w_hbm, w_buf, load_sem.at[1])
    load_z.start()
    load_w.start()

    with jax.named_scope("local_terms"):
        gates(gl_ref, bl_ref, rate_ref, k_ref, q_ref, s)
        block_terms(k_ref, q_ref, v_ref, s)
        run_shard(s)

    pl.semaphore_wait(barrier, len(peers))
    sends = []

    def go(copy):
        copy.start()
        sends.append(copy)

    for i in range(1, NY):
        to = (y + i) % NY
        go(remote(msg.at[to], dball.at[y, z], y_send.at[i - 1], y_recv.at[i - 1], at(to, z)))
    dball[y, z] = msg[y]
    block_output(0, q_ref, s)
    for i in range(1, NY):
        remote(msg.at[0], dball.at[(y + NY - i) % NY, z], y_send.at[i - 1], y_recv.at[i - 1], at(y, z)).wait_recv()

    for i in range(1, NZ):
        to = (z + i) % NZ
        piece = pl.ds(pl.multiple_of(ROWS_C + 16 * to, 16), 16)
        go(remote(dball.at[:, z, piece, :], bst.at[:, z], b_send.at[i - 1], b_recv.at[i - 1], at(y, to)))
    own = pl.ds(pl.multiple_of(ROWS_C + 16 * z, 16), 16)
    for r in range(NY):
        bst[r, z] = dball[r, z, own, :]

    right, left = (z + 1) % NZ, (z + NZ - 1) % NZ

    def ring(level):
        for r in range(NY):
            if level < 4 or r % 2 == 0:
                slot = dball.at[r, (z + NZ - level + 1) % NZ, :ROWS_C, :]
                go(remote(slot, slot, rr_send.at[level - 1, r], rr_recv.at[level - 1, r], at(y, right)))
            if level < 4 or r % 2 == 1:
                slot = dball.at[r, (z + level - 1) % NZ, :ROWS_C, :]
                go(remote(slot, slot, rl_send.at[level - 1, r], rl_recv.at[level - 1, r], at(y, left)))

    def ring_wait(level):
        for r in range(NY):
            if level < 4 or r % 2 == 0:
                slot = dball.at[r, (z + NZ - level) % NZ, :ROWS_C, :]
                remote(slot, slot, rr_send.at[level - 1, r], rr_recv.at[level - 1, r], at(y, right)).wait_recv()
            if level < 4 or r % 2 == 1:
                slot = dball.at[r, (z + level) % NZ, :ROWS_C, :]
                remote(slot, slot, rl_send.at[level - 1, r], rl_recv.at[level - 1, r], at(y, left)).wait_recv()

    ring(1)
    for level in range(1, 4):
        block_output(level, q_ref, s)
        ring_wait(level)
        ring(level + 1)
    load_z.wait()
    zf = z_buf[...].astype(F32)
    zs = zf * sigmoid(zf)
    for h in range(NH):
        gate[:, BLK * h : BLK * (h + 1)] = zs[:, BLK * h : BLK * (h + 1)] * gain_ref[...]
    ring_wait(4)
    for i in range(1, NZ):
        remote(
            dball.at[:, z, :16, :], bst.at[:, (z + NZ - i) % NZ], b_send.at[i - 1], b_recv.at[i - 1], at(y, z)
        ).wait_recv()

    carry = jnp.zeros((16, BLK), F32)
    for r in range(NY):
        for j in range(NZ):
            xst[r, j] = carry.astype(BF16)
            if r == NY - 1 and j == NZ - 1:
                break
            c = jnp.sum(dball[r, j, ROWS_D:ROWS_C, :].astype(F32), axis=0, keepdims=True)
            carry = c * carry - dot(carry.astype(BF16), dball[r, j, :ROWS_D, :]) + bst[r, j].astype(F32)

        @pl.when(y != r)
        def _():
            remote(xst.at[r], xr.at[y], u_send.at[r], u_recv.at[y], at(r, z)).start()

        @pl.when(y == r)
        def _():
            xr[y] = xst[r]

    for i in range(1, NY):
        source = (y + i) % NY
        remote(xst.at[0], xr.at[source], u_send.at[0], u_recv.at[source], at(y, z)).wait_recv()
    for i in range(1, NZ):
        to = (z + i) % NZ
        go(remote(xr.at[:, to], xin.at[:, z], x_send.at[i - 1], x_recv.at[i - 1], at(y, to)))
    for h in range(NH):
        xin[h, z] = xr[h, z]
    for i in range(1, NZ):
        remote(
            xr.at[:, z], xin.at[:, (z + NZ - i) % NZ], x_send.at[i - 1], x_recv.at[i - 1], at(y, z)
        ).wait_recv()

    load_w.wait()

    def gate_half(which):
        for h in range(NH):
            start = xin[h].reshape(BLK, BLK)
            for j in range(NX):
                tok = pl.ds(pl.multiple_of((2 * j + which) * 64, 64), 64)
                core_out = oloc[h, tok, :] + dot_nt(corr[h, tok, :], start)
                r = rq[h // 2, tok, :]
                mean = jnp.mean(core_out * core_out, axis=1, keepdims=True)
                scale = r * lax.rsqrt(r * r * mean + 1e-06)
                lanes = slice(BLK * h, BLK * (h + 1))
                gated[64 * j : 64 * (j + 1), lanes] = (core_out * scale * gate[tok, lanes]).astype(BF16)

    gate_half(1 - core)
    for n in range(4):
        parta[n] = dot(gated[...], w_buf[:, 512 * n : 512 * (n + 1)]).astype(BF16)
        go(remote(parta.at[n], recva.at[n], a_send.at[n], a_recv.at[n], on_line(x, 1 - core)))
    gate_half(core)
    for n in range(4):
        partb[n] = dot(gated[...], w_buf[:, 512 * n : 512 * (n + 1)])
        remote(parta.at[n], recva.at[n], a_send.at[n], a_recv.at[n], on_line(x, core)).wait_recv()
        partb[n] = partb[n] + recva[n].astype(F32)
        sumb[n] = partb[n].astype(BF16)
        for i in range(1, NX):
            to = (x + i) % NX
            rows_to = pl.ds(pl.multiple_of(64 * to, 64), 64)
            go(remote(sumb.at[n, rows_to, :], recvb.at[n, i - 1], e_send.at[n, i - 1], e_recv.at[n, i - 1], on_line(to, core)))
    mine = pl.ds(pl.multiple_of(64 * x, 64), 64)
    for n in range(4):
        total = partb[n, mine, :]
        for i in range(1, NX):
            remote(
                sumb.at[n, mine, :], recvb.at[n, i - 1], e_send.at[n, i - 1], e_recv.at[n, i - 1], on_line(x, core)
            ).wait_recv()
            total = total + recvb[n, i - 1].astype(F32)
        out_ref[:, 512 * n : 512 * (n + 1)] = total.astype(BF16)

    for copy in sends:
        copy.wait_send()
    for r in range(NY):

        @pl.when(y != r)
        def _():
            remote(xst.at[r], xr.at[y], u_send.at[r], u_recv.at[y], at(r, z)).wait_send()


def on_device(query, keys, values, gate_logit, beta_logit, decay_rate, norm_gain, gate_z, out_weight):
    vmem = pl.BlockSpec(memory_space=pltpu.VMEM)
    anywhere = pl.BlockSpec(memory_space=pl.ANY)
    dma = pltpu.SemaphoreType.DMA
    pairs = NB * NH
    scratch = [
        pltpu.VMEM((16, BLK), F32),
        pltpu.VMEM((NB, 32, BLK), F32),
        pltpu.VMEM((NB, BLK, 32), F32),
        pltpu.VMEM((2, 512, 1), F32),
        pltpu.VMEM((2 * NB, BLK, BLK), BF16),
        pltpu.VMEM((pairs, BLK, BLK), BF16),
        pltpu.VMEM((8, BLK, BLK), F32),
        pltpu.VMEM((8, BLK, BLK), F32),
        pltpu.VMEM((pairs, BLK, BLK), F32),
        pltpu.VMEM((pairs, BLK, BLK), BF16),
        pltpu.VMEM((NH, BLK, 2 * BLK), F32),
        pltpu.VMEM((pairs, BLK, 2 * BLK), BF16),
        pltpu.VMEM((pairs, BLK, 2 * BLK), BF16),
        pltpu.VMEM((NH, BLK, 2 * BLK), BF16),
        pltpu.VMEM((NH, ROWS_M, BLK), BF16),
        pltpu.VMEM((NH, 512, BLK), F32),
        pltpu.VMEM((NH, 512, BLK), BF16),
        pltpu.VMEM((512, 512), BF16),
        pltpu.VMEM((512, 2048), BF16),
        pltpu.VMEM((512, 512), F32),
        pltpu.VMEM((NY, NZ, ROWS_M, BLK), BF16),
        pltpu.VMEM((NY, NZ, 16, BLK), BF16),
        pltpu.VMEM((NY, NZ, 16, BLK), BF16),
        pltpu.VMEM((NH, NZ, 16, BLK), BF16),
        pltpu.VMEM((NH, NZ, 16, BLK), BF16),
        pltpu.VMEM((256, 512), BF16),
        pltpu.VMEM((4, 256, 512), BF16),
        pltpu.VMEM((4, 256, 512), BF16),
        pltpu.VMEM((4, 256, 512), F32),
        pltpu.VMEM((4, 256, 512), BF16),
        pltpu.VMEM((4, 3, 64, 512), BF16),
        dma((2,)),
        dma((3,)), dma((3,)),
        dma((4, 4)), dma((4, 4)), dma((4, 4)), dma((4, 4)),
        dma((7,)), dma((7,)),
        dma((4,)), dma((4,)),
        dma((7,)), dma((7,)),
        dma((4,)), dma((4,)),
        dma((4, 3)), dma((4, 3)),
    ]
    return pl.pallas_call(
        kernel,
        out_shape=jax.ShapeDtypeStruct((64, 2048), BF16),
        in_specs=[vmem] * 7 + [anywhere] * 2,
        out_specs=vmem,
        scratch_shapes=scratch,
        compiler_params=pltpu.CompilerParams(
            collective_id=0, has_side_effects=True, vmem_limit_bytes=48 * 1024 * 1024
        ),
    )(
        query, keys, values, gate_logit.T, beta_logit.T, decay_rate.reshape(NH, 1),
        norm_gain.reshape(1, BLK), gate_z, out_weight,
    )


def solution(mesh):
    return jax.shard_map(
        on_device,
        mesh=mesh,
        in_specs=(
            P("seq", "head"),
            P("seq", "head"),
            P("seq", "head"),
            P("seq", "head"),
            P("seq", "head"),
            P("head"),
            P(),
            P("seq", "head"),
            P("head", None),
        ),
        out_specs=P(("seq", "head"), None),
        check_vma=False,
    )
```

time: 650 us -> 80.4 us (0.12)
  the two profiles are of different devices: /device:TPU:60 before, /device:TPU:24 now
where the time goes in v1:
time: 80.4 us; the launch traced here: 80 us
  Pallas kernels  70.9 us (88%)
  local copies, waits for them, and re-layouts  9.06 us (11%)
    pallas_call x1, Pallas kernels, on_device(): pl.pallas_call(kernel, out_shape=jax.ShapeDtypeStruct((64, 2048), BF16),...  70.9 us
    unnamed x17, local copies, waits for them, and re-layouts  8.32 us

profile of v1, /device:TPU:24, one launch (start us, length us, event | category | flops | bytes accessed | tf_op | source)
XLA Modules:
  0.0 80.0 jit_solution(10041611696845911950)
XLA Ops:
  0.0 0.7 copy.10.rate_ref
  0.7 0.0 copy-start
  0.7 1.6 %copy-done = bf16[512,2048]{1,0:T(8,128)(2,1)S(1)} copy-done((bf16[512,2048]{1,0:T(8,128)(2,1)S(1)}, bf16[512,2048]{1,0:T(8,128)(2,1)}, u32[]{:S(2)}) %copy-start) | copy-done | bytes 2097176
  2.3 0.0 copy-start.1
  2.3 1.0 %copy-done.1 = bf16[512,512]{1,0:T(8,128)(2,1)S(1)} copy-done((bf16[512,512]{1,0:T(8,128)(2,1)S(1)}, bf16[512,512]{1,0:T(8,128)(2,1)}, u32[]{:S(2)}) %copy-start.1) | copy-done | bytes 524312
  3.4 0.0 copy-start.2
  3.4 1.0 %copy-done.2 = bf16[512,512]{1,0:T(8,128)(2,1)S(1)} copy-done((bf16[512,512]{1,0:T(8,128)(2,1)S(1)}, bf16[512,512]{1,0:T(8,128)(2,1)}, u32[]{:S(2)}) %copy-start.2) | copy-done | bytes 524312
  4.4 0.0 copy-start.3
  4.4 0.9 %copy-done.3 = bf16[512,256]{1,0:T(8,128)(2,1)S(1)} copy-done((bf16[512,256]{1,0:T(8,128)(2,1)S(1)}, bf16[512,256]{1,0:T(8,128)(2,1)}, u32[]{:S(2)}) %copy-start.3) | copy-done | bytes 262168
  5.4 0.0 copy-start.4
  5.4 0.9 %copy-done.4 = bf16[512,256]{1,0:T(8,128)(2,1)S(1)} copy-done((bf16[512,256]{1,0:T(8,128)(2,1)S(1)}, bf16[512,256]{1,0:T(8,128)(2,1)}, u32[]{:S(2)}) %copy-start.4) | copy-done | bytes 262168
  6.3 0.0 copy-start.5
  6.3 0.7 copy-done.5
  7.0 0.0 copy-start.6
  7.0 0.7 copy-done.6
  7.7 0.0 copy-start.7
  7.7 0.7 copy-done.7
  8.4 70.9 %shard_map.91 = bf16[64,2048]{1,0:T(8,128)(2,1)S(1)} custom-call(bf16[512,256]{1,0:T(8,128)(2,1)S(1)} %copy-done.3, bf16[512,256]{1,0:T(8,128)(2,1)S(1)} %copy-done.4, bf16[512,512]{1,0:T(8,128)(2,1)S(1)} %copy-done.1, f32[4,512]{1,0:T(4,128)S(1)} %bitcast.4, f32[4,512]{1,0:T(4,128)S(1)} %bitcast.5, f32[4,1]{1,0:T(4,128)S(1)} %copy.10.rate_ref, ...), custom_call_target="tpu_custom_call" | custom-call | tf_op jit(solution)/shard_map/pallas_call | solution.py:419
  79.3 0.7 copy.12
Async XLA Ops:
  0.7 1.6 %copy-start = (bf16[512,2048]{1,0:T(8,128)(2,1)S(1)}, bf16[512,2048]{1,0:T(8,128)(2,1)}, u32[]{:S(2)}) copy-start(bf16[512,2048]{1,0:T(8,128)(2,1)} %w_hbm.1) | copy-start | bytes 6291460
  2.3 1.0 %copy-start.1 = (bf16[512,512]{1,0:T(8,128)(2,1)S(1)}, bf16[512,512]{1,0:T(8,128)(2,1)}, u32[]{:S(2)}) copy-start(bf16[512,512]{1,0:T(8,128)(2,1)} %v_ref.1) | copy-start | bytes 1572868
  3.4 1.0 %copy-start.2 = (bf16[512,512]{1,0:T(8,128)(2,1)S(1)}, bf16[512,512]{1,0:T(8,128)(2,1)}, u32[]{:S(2)}) copy-start(bf16[512,512]{1,0:T(8,128)(2,1)} %z_hbm.1) | copy-start | bytes 1572868
  4.4 0.9 %copy-start.3 = (bf16[512,256]{1,0:T(8,128)(2,1)S(1)}, bf16[512,256]{1,0:T(8,128)(2,1)}, u32[]{:S(2)}) copy-start(bf16[512,256]{1,0:T(8,128)(2,1)} %q_ref.1) | copy-start | bytes 786436
  5.4 0.9 %copy-start.4 = (bf16[512,256]{1,0:T(8,128)(2,1)S(1)}, bf16[512,256]{1,0:T(8,128)(2,1)}, u32[]{:S(2)}) copy-start(bf16[512,256]{1,0:T(8,128)(2,1)} %k_ref.1) | copy-start | bytes 786436
  6.3 0.7 copy-start.5
  7.0 0.7 copy-start.6
  7.7 0.7 copy-start.7

commit v2 on v1

--- a/solution.py
+++ b/solution.py
@@ -14,6 +14,9 @@
 ROWS_D = 128
 ROWS_C = 144
 ROWS_M = 272
+TREE = (
+    (0, 0, None), (4, 0, 12), (2, 0, 8), (1, 0, 0), (6, 4, 10), (5, 4, 4), (3, 2, 2), (7, 6, 6),
+)
 F32 = jnp.float32
 BF16 = jnp.bfloat16
 
@@ -45,7 +48,9 @@
 
 
 def gates(gl_ref, bl_ref, rate_ref, k_ref, q_ref, s):
-    g4 = -rate_ref[...] * softplus(gl_ref[...])
+    same = lax.broadcasted_iota(jnp.int32, (NH, NH), 0) == lax.broadcasted_iota(jnp.int32, (NH, NH), 1)
+    rate = jnp.sum(jnp.where(same, rate_ref[...], 0.0), axis=1, keepdims=True)
+    g4 = -rate * softplus(gl_ref[...])
     beta4 = sigmoid(bl_ref[...])
     for b in range(NB):
         s["g16"][pl.ds(4 * b, 4), :] = g4[:, BLK * b : BLK * (b + 1)]
@@ -164,18 +169,32 @@
         return carry
 
     lax.fori_loop(0, NB, block, 0)
+
+
+def write_message(ref, c, fix, inject):
     c_ids = lax.broadcasted_iota(jnp.int32, (16, BLK), 0)
-    for h in range(NH):
-        total = s["g16"][pl.ds(h, 1), :]
-        for b in range(1, NB):
-            total = total + s["g16"][pl.ds(4 * b + h, 1), :]
-        c = jnp.exp(jnp.broadcast_to(total[:, BLK - 1 : BLK], (16, BLK)))
-        hi, mid, low = (part.astype(F32) for part in split3(c))
-        terms = jnp.where(c_ids == 0, hi, jnp.where(c_ids == 1, mid, jnp.where(c_ids == 2, low, 0.0)))
-        fix = jnp.where(eye, c[:1], 0.0) - s["state"][h, :, BLK:]
-        s["msg"][h, :ROWS_D, :] = fix.T.astype(BF16)
-        s["msg"][h, ROWS_D:ROWS_C, :] = terms.astype(BF16)
-        s["msg"][h, ROWS_C:, :] = s["state"][h, :, :BLK].T.astype(BF16)
+    hi, mid, low = (part.astype(F32) for part in split3(jnp.broadcast_to(c, (16, BLK))))
+    terms = jnp.where(c_ids == 0, hi, jnp.where(c_ids == 1, mid, jnp.where(c_ids == 2, low, 0.0)))
+    ref[:ROWS_D, :] = fix.astype(BF16)
+    ref[ROWS_D:ROWS_C, :] = terms.astype(BF16)
+    ref[ROWS_C:, :] = inject.astype(BF16)
+
+
+def decay_of(ref):
+    return jnp.sum(ref[ROWS_D:ROWS_C, :].astype(F32), axis=0, keepdims=True)
+
+
+def compose(first, second, out):
+    c_1, c_2 = decay_of(first), decay_of(second)
+    prod = dot(first[...], second[:ROWS_D, :])
+    fix = c_2 * first[:ROWS_D, :].astype(F32) + c_1 * second[:ROWS_D, :].astype(F32) - prod[:ROWS_D]
+    inject = c_2 * first[ROWS_C:, :].astype(F32) + second[ROWS_C:, :].astype(F32) - prod[ROWS_C:]
+    write_message(out, c_1 * c_2, fix, inject)
+
+
+def step(ref, state):
+    moved = decay_of(ref) * state - dot(state.astype(BF16), ref[:ROWS_D, :])
+    return moved + ref[ROWS_C:, :].astype(F32)
 
 
 def block_output(b, q_ref, s):
@@ -190,23 +209,39 @@
 
 
 def kernel(
-    q_ref, k_ref, v_ref, gl_ref, bl_ref, rate_ref, gain_ref, z_hbm, w_hbm, out_ref,
+    q_hbm, k_hbm, v_hbm, gl_hbm, bl_hbm, rate_hbm, gain_hbm, z_hbm, w_hbm, out_ref,
+    q_ref, k_ref, v_ref, gl_ref, bl_ref, rate_ref, gain_ref, z_buf, w_buf,
     g16, rows, cols, rq, kt, mix, low, inv, upd, wts, state, sb, rb, re, msg, oloc, corr,
-    z_buf, w_buf, gate, dball, bst, xst, xr, xin, gated, parta, recva, partb, sumb, recvb,
-    load_sem, y_send, y_recv, rr_send, rr_recv, rl_send, rl_recv, b_send, b_recv,
-    u_send, u_recv, x_send, x_recv, a_send, a_recv, e_send, e_recv,
+    gate, parts, rmsg, rowbuf, start, xst, xin,
+    gated, parta, recva, partb, sumb, relay, hop, recvb,
+    load_sem, m_send, m_recv, r_send, r_recv, x_send, x_recv,
+    a_send, a_recv, f_send, f_recv, e_send, e_recv,
 ):
     s = dict(
         g16=g16, rows=rows, cols=cols, rq=rq, kt=kt, mix=mix, low=low, inv=inv, upd=upd, wts=wts,
         state=state, sb=sb, rb=rb, re=re, msg=msg, oloc=oloc, corr=corr,
     )
+    loads = [
+        pltpu.make_async_copy(src, dst, load_sem.at[i])
+        for i, (src, dst) in enumerate([
+            (gl_hbm, gl_ref), (bl_hbm, bl_ref), (rate_hbm, rate_ref), (k_hbm, k_ref), (q_hbm, q_ref),
+            (v_hbm, v_ref), (gain_hbm, gain_ref), (z_hbm, z_buf), (w_hbm, w_buf),
+        ])
+    ]
+    for load in loads:
+        load.start()
     seq = lax.axis_index("seq")
     head = lax.axis_index("head")
     y, z = seq // NZ, seq % NZ
     x, core = head // 2, head % 2
+    mine = z // 2
+    owns = z % 2 == core
 
     def at(y_to, z_to):
         return (y_to * NZ + z_to, head)
+
+    def owner(h):
+        return at(y, 2 * h + core)
 
     def on_line(x_to, core_to):
         return (seq, 2 * x_to + core_to)
@@ -217,23 +252,19 @@
             device_id=device, device_id_type=pl.DeviceIdType.MESH,
         )
 
-    peers = [at((y + i) % NY, z) for i in range(1, NY)]
-    peers += [at(y, (z + i) % NZ) for i in range(1, NZ)]
-    peers += [on_line((x + i) % NX, core) for i in range(1, NX)]
-    peers += [on_line(x, 1 - core)]
+    ahead, behind = (x + 1) % NX, (x + NX - 1) % NX
+    peers = [at(y, (z + i) % NZ) for i in range(1, NZ)]
+    peers += [at((y + i) % NY, z) for i in range(1, NY)]
+    peers += [on_line(ahead, core), on_line(behind, core), on_line(x, 1 - core)]
     barrier = pltpu.get_barrier_semaphore()
     for peer in peers:
         pl.semaphore_signal(barrier, inc=1, device_id=peer, device_id_type=pl.DeviceIdType.MESH)
-    load_z = pltpu.make_async_copy(z_hbm, z_buf, load_sem.at[0])
-    load_w = pltpu.make_async_copy(w_hbm, w_buf, load_sem.at[1])
-    load_z.start()
-    load_w.start()
-
-    with jax.named_scope("local_terms"):
-        gates(gl_ref, bl_ref, rate_ref, k_ref, q_ref, s)
-        block_terms(k_ref, q_ref, v_ref, s)
-        run_shard(s)
-
+    for load in loads[:6]:
+        load.wait()
+
+    gates(gl_ref, bl_ref, rate_ref, k_ref, q_ref, s)
+    block_terms(k_ref, q_ref, v_ref, s)
+    run_shard(s)
     pl.semaphore_wait(barrier, len(peers))
     sends = []
 
@@ -241,141 +272,172 @@
         copy.start()
         sends.append(copy)
 
-    for i in range(1, NY):
-        to = (y + i) % NY
-        go(remote(msg.at[to], dball.at[y, z], y_send.at[i - 1], y_recv.at[i - 1], at(to, z)))
-    dball[y, z] = msg[y]
-    block_output(0, q_ref, s)
-    for i in range(1, NY):
-        remote(msg.at[0], dball.at[(y + NY - i) % NY, z], y_send.at[i - 1], y_recv.at[i - 1], at(y, z)).wait_recv()
-
-    for i in range(1, NZ):
-        to = (z + i) % NZ
-        piece = pl.ds(pl.multiple_of(ROWS_C + 16 * to, 16), 16)
-        go(remote(dball.at[:, z, piece, :], bst.at[:, z], b_send.at[i - 1], b_recv.at[i - 1], at(y, to)))
-    own = pl.ds(pl.multiple_of(ROWS_C + 16 * z, 16), 16)
-    for r in range(NY):
-        bst[r, z] = dball[r, z, own, :]
-
-    right, left = (z + 1) % NZ, (z + NZ - 1) % NZ
-
-    def ring(level):
-        for r in range(NY):
-            if level < 4 or r % 2 == 0:
-                slot = dball.at[r, (z + NZ - level + 1) % NZ, :ROWS_C, :]
-                go(remote(slot, slot, rr_send.at[level - 1, r], rr_recv.at[level - 1, r], at(y, right)))
-            if level < 4 or r % 2 == 1:
-                slot = dball.at[r, (z + level - 1) % NZ, :ROWS_C, :]
-                go(remote(slot, slot, rl_send.at[level - 1, r], rl_recv.at[level - 1, r], at(y, left)))
-
-    def ring_wait(level):
-        for r in range(NY):
-            if level < 4 or r % 2 == 0:
-                slot = dball.at[r, (z + NZ - level) % NZ, :ROWS_C, :]
-                remote(slot, slot, rr_send.at[level - 1, r], rr_recv.at[level - 1, r], at(y, right)).wait_recv()
-            if level < 4 or r % 2 == 1:
-                slot = dball.at[r, (z + level) % NZ, :ROWS_C, :]
-                remote(slot, slot, rl_send.at[level - 1, r], rl_recv.at[level - 1, r], at(y, left)).wait_recv()
-
-    ring(1)
-    for level in range(1, 4):
-        block_output(level, q_ref, s)
-        ring_wait(level)
-        ring(level + 1)
-    load_z.wait()
+    row_ids = lax.broadcasted_iota(jnp.int32, (BLK, BLK), 0)
+    eye = row_ids == lax.broadcasted_iota(jnp.int32, (BLK, BLK), 1)
+    for h in range(NH):
+        total = g16[pl.ds(h, 1), :]
+        for b in range(1, NB):
+            total = total + g16[pl.ds(4 * b + h, 1), :]
+        c = jnp.exp(jnp.broadcast_to(total[:, BLK - 1 : BLK], (1, BLK)))
+        fix = jnp.where(eye, c, 0.0) - state[h, :, BLK:]
+        write_message(msg.at[h], c, fix.T, state[h, :, :BLK].T)
+
+        @pl.when(z != 2 * h + core)
+        def _():
+            remote(msg.at[h], parts.at[z], m_send.at[h], m_recv.at[z], owner(h)).start()
+
+        @pl.when(z == 2 * h + core)
+        def _():
+            parts[z] = msg[h]
+
+    for b in range(NB):
+        block_output(b, q_ref, s)
+    for load in loads[6:]:
+        load.wait()
     zf = z_buf[...].astype(F32)
     zs = zf * sigmoid(zf)
     for h in range(NH):
         gate[:, BLK * h : BLK * (h + 1)] = zs[:, BLK * h : BLK * (h + 1)] * gain_ref[...]
-    ring_wait(4)
-    for i in range(1, NZ):
-        remote(
-            dball.at[:, z, :16, :], bst.at[:, (z + NZ - i) % NZ], b_send.at[i - 1], b_recv.at[i - 1], at(y, z)
-        ).wait_recv()
-
-    carry = jnp.zeros((16, BLK), F32)
-    for r in range(NY):
-        for j in range(NZ):
-            xst[r, j] = carry.astype(BF16)
-            if r == NY - 1 and j == NZ - 1:
-                break
-            c = jnp.sum(dball[r, j, ROWS_D:ROWS_C, :].astype(F32), axis=0, keepdims=True)
-            carry = c * carry - dot(carry.astype(BF16), dball[r, j, :ROWS_D, :]) + bst[r, j].astype(F32)
-
-        @pl.when(y != r)
+
+    @pl.when(owns)
+    def _():
+        for k in range(4):
+            for j in (2 * k, 2 * k + 1):
+
+                @pl.when(z != j)
+                def _():
+                    remote(msg.at[0], parts.at[j], m_send.at[0], m_recv.at[j], at(y, z)).wait_recv()
+
+            compose(parts.at[2 * k], parts.at[2 * k + 1], parts.at[8 + k])
+        for k in range(2):
+            compose(parts.at[8 + 2 * k], parts.at[9 + 2 * k], parts.at[12 + k])
+        compose(parts.at[12], parts.at[13], rmsg)
+        for i in range(NY - 1, 0, -1):
+
+            @pl.when(y + i < NY)
+            def _():
+                remote(rmsg, rowbuf.at[y], r_send.at[i - 1], r_recv.at[y], at((y + i) % NY, z)).start()
+
+        start[...] = jnp.zeros_like(start)
+        for r in range(NY - 1):
+
+            @pl.when(r < y)
+            def _():
+                remote(rmsg, rowbuf.at[r], r_send.at[0], r_recv.at[r], at(y, z)).wait_recv()
+                if r == 0:
+                    start[...] = rowbuf[r, ROWS_C:, :].astype(F32)
+                else:
+                    start[...] = step(rowbuf.at[r], start[...])
+
+        states = {0: start[...]}
+        for j, source, stretch in TREE:
+            if stretch is not None:
+                states[j] = step(parts.at[stretch], states[source])
+            xst[j] = states[j].astype(BF16)
+
+            @pl.when(j != z)
+            def _():
+                remote(xst.at[j], xin.at[mine], x_send.at[j], x_recv.at[mine], at(y, j)).start()
+
+            @pl.when(j == z)
+            def _():
+                xin[mine] = xst[j]
+
+    for h in range(NH):
+
+        @pl.when(z != 2 * h + core)
         def _():
-            remote(xst.at[r], xr.at[y], u_send.at[r], u_recv.at[y], at(r, z)).start()
-
-        @pl.when(y == r)
-        def _():
-            xr[y] = xst[r]
-
-    for i in range(1, NY):
-        source = (y + i) % NY
-        remote(xst.at[0], xr.at[source], u_send.at[0], u_recv.at[source], at(y, z)).wait_recv()
-    for i in range(1, NZ):
-        to = (z + i) % NZ
-        go(remote(xr.at[:, to], xin.at[:, z], x_send.at[i - 1], x_recv.at[i - 1], at(y, to)))
-    for h in range(NH):
-        xin[h, z] = xr[h, z]
-    for i in range(1, NZ):
-        remote(
-            xr.at[:, z], xin.at[:, (z + NZ - i) % NZ], x_send.at[i - 1], x_recv.at[i - 1], at(y, z)
-        ).wait_recv()
-
-    load_w.wait()
+            remote(xst.at[0], xin.at[h], x_send.at[0], x_recv.at[h], at(y, z)).wait_recv()
 
     def gate_half(which):
         for h in range(NH):
-            start = xin[h].reshape(BLK, BLK)
             for j in range(NX):
                 tok = pl.ds(pl.multiple_of((2 * j + which) * 64, 64), 64)
-                core_out = oloc[h, tok, :] + dot_nt(corr[h, tok, :], start)
+                core_out = oloc[h, tok, :] + dot_nt(corr[h, tok, :], xin[h])
                 r = rq[h // 2, tok, :]
                 mean = jnp.mean(core_out * core_out, axis=1, keepdims=True)
                 scale = r * lax.rsqrt(r * r * mean + 1e-06)
                 lanes = slice(BLK * h, BLK * (h + 1))
                 gated[64 * j : 64 * (j + 1), lanes] = (core_out * scale * gate[tok, lanes]).astype(BF16)
 
+    order = (0, 2, 1, 3)
     gate_half(1 - core)
-    for n in range(4):
+    for n in order:
         parta[n] = dot(gated[...], w_buf[:, 512 * n : 512 * (n + 1)]).astype(BF16)
         go(remote(parta.at[n], recva.at[n], a_send.at[n], a_recv.at[n], on_line(x, 1 - core)))
     gate_half(core)
-    for n in range(4):
+
+    def rows_of(chip):
+        return pl.ds(pl.multiple_of(64 * chip, 64), 64)
+
+    def ways(n):
+        return (ahead, behind) if n < 2 else (behind, ahead)
+
+    def send_on(n):
+        onward, back = ways(n)
+        remote(sumb.at[n, rows_of(x), :], relay.at[n], f_send.at[n], f_recv.at[n], on_line(x, core)).wait_recv()
+        hop[n] = (partb[n, rows_of(onward), :] + relay[n].astype(F32)).astype(BF16)
+        go(remote(hop.at[n], recvb.at[n, 1], e_send.at[n, 1], e_recv.at[n, 1], on_line(onward, core)))
+
+    for count, n in enumerate(order):
+        onward, back = ways(n)
         partb[n] = dot(gated[...], w_buf[:, 512 * n : 512 * (n + 1)])
         remote(parta.at[n], recva.at[n], a_send.at[n], a_recv.at[n], on_line(x, core)).wait_recv()
         partb[n] = partb[n] + recva[n].astype(F32)
         sumb[n] = partb[n].astype(BF16)
-        for i in range(1, NX):
-            to = (x + i) % NX
-            rows_to = pl.ds(pl.multiple_of(64 * to, 64), 64)
-            go(remote(sumb.at[n, rows_to, :], recvb.at[n, i - 1], e_send.at[n, i - 1], e_recv.at[n, i - 1], on_line(to, core)))
-    mine = pl.ds(pl.multiple_of(64 * x, 64), 64)
-    for n in range(4):
-        total = partb[n, mine, :]
-        for i in range(1, NX):
+        far = rows_of((x + 2) % NX)
+        go(remote(sumb.at[n, far, :], relay.at[n], f_send.at[n], f_recv.at[n], on_line(onward, core)))
+        go(remote(sumb.at[n, rows_of(back), :], recvb.at[n, 0], e_send.at[n, 0], e_recv.at[n, 0], on_line(back, core)))
+        if count >= 2:
+            send_on(order[count - 2])
+    send_on(order[2])
+    send_on(order[3])
+    for n in order:
+        total = partb[n, rows_of(x), :]
+        for i in range(2):
             remote(
-                sumb.at[n, mine, :], recvb.at[n, i - 1], e_send.at[n, i - 1], e_recv.at[n, i - 1], on_line(x, core)
+                hop.at[n], recvb.at[n, i], e_send.at[n, i], e_recv.at[n, i], on_line(x, core)
             ).wait_recv()
-            total = total + recvb[n, i - 1].astype(F32)
+            total = total + recvb[n, i].astype(F32)
         out_ref[:, 512 * n : 512 * (n + 1)] = total.astype(BF16)
 
     for copy in sends:
         copy.wait_send()
-    for r in range(NY):
-
-        @pl.when(y != r)
+    for h in range(NH):
+
+        @pl.when(z != 2 * h + core)
         def _():
-            remote(xst.at[r], xr.at[y], u_send.at[r], u_recv.at[y], at(r, z)).wait_send()
+            remote(msg.at[h], parts.at[z], m_send.at[h], m_recv.at[z], owner(h)).wait_send()
+
+    @pl.when(owns)
+    def _():
+        for j in range(NZ):
+
+            @pl.when(j != z)
+            def _():
+                remote(xst.at[j], xin.at[mine], x_send.at[j], x_recv.at[mine], at(y, j)).wait_send()
+
+        for i in range(1, NY):
+
+            @pl.when(y + i < NY)
+            def _():
+                remote(rmsg, rowbuf.at[y], r_send.at[i - 1], r_recv.at[y], at((y + i) % NY, z)).wait_send()
 
 
 def on_device(query, keys, values, gate_logit, beta_logit, decay_rate, norm_gain, gate_z, out_weight):
-    vmem = pl.BlockSpec(memory_space=pltpu.VMEM)
-    anywhere = pl.BlockSpec(memory_space=pl.ANY)
+    hbm = pl.BlockSpec(memory_space=pltpu.HBM)
     dma = pltpu.SemaphoreType.DMA
     pairs = NB * NH
     scratch = [
+        pltpu.VMEM((512, 256), BF16),
+        pltpu.VMEM((512, 256), BF16),
+        pltpu.VMEM((512, 512), BF16),
+        pltpu.VMEM((NH, 512), F32),
+        pltpu.VMEM((NH, 512), F32),
+        pltpu.VMEM((1, NH), F32),
+        pltpu.VMEM((1, BLK), F32),
+        pltpu.VMEM((512, 512), BF16),
+        pltpu.VMEM((512, 2048), BF16),
         pltpu.VMEM((16, BLK), F32),
         pltpu.VMEM((NB, 32, BLK), F32),
         pltpu.VMEM((NB, BLK, 32), F32),
@@ -393,40 +455,40 @@
         pltpu.VMEM((NH, ROWS_M, BLK), BF16),
         pltpu.VMEM((NH, 512, BLK), F32),
         pltpu.VMEM((NH, 512, BLK), BF16),
-        pltpu.VMEM((512, 512), BF16),
-        pltpu.VMEM((512, 2048), BF16),
         pltpu.VMEM((512, 512), F32),
-        pltpu.VMEM((NY, NZ, ROWS_M, BLK), BF16),
-        pltpu.VMEM((NY, NZ, 16, BLK), BF16),
-        pltpu.VMEM((NY, NZ, 16, BLK), BF16),
-        pltpu.VMEM((NH, NZ, 16, BLK), BF16),
-        pltpu.VMEM((NH, NZ, 16, BLK), BF16),
+        pltpu.VMEM((14, ROWS_M, BLK), BF16),
+        pltpu.VMEM((ROWS_M, BLK), BF16),
+        pltpu.VMEM((NY, ROWS_M, BLK), BF16),
+        pltpu.VMEM((BLK, BLK), F32),
+        pltpu.VMEM((NZ, BLK, BLK), BF16),
+        pltpu.VMEM((NH, BLK, BLK), BF16),
         pltpu.VMEM((256, 512), BF16),
         pltpu.VMEM((4, 256, 512), BF16),
         pltpu.VMEM((4, 256, 512), BF16),
         pltpu.VMEM((4, 256, 512), F32),
         pltpu.VMEM((4, 256, 512), BF16),
-        pltpu.VMEM((4, 3, 64, 512), BF16),
-        dma((2,)),
-        dma((3,)), dma((3,)),
-        dma((4, 4)), dma((4, 4)), dma((4, 4)), dma((4, 4)),
-        dma((7,)), dma((7,)),
+        pltpu.VMEM((4, 64, 512), BF16),
+        pltpu.VMEM((4, 64, 512), BF16),
+        pltpu.VMEM((4, 2, 64, 512), BF16),
+        dma((9,)),
+        dma((4,)), dma((8,)),
+        dma((3,)), dma((4,)),
+        dma((8,)), dma((4,)),
         dma((4,)), dma((4,)),
-        dma((7,)), dma((7,)),
         dma((4,)), dma((4,)),
-        dma((4, 3)), dma((4, 3)),
+        dma((4, 2)), dma((4, 2)),
     ]
     return pl.pallas_call(
         kernel,
         out_shape=jax.ShapeDtypeStruct((64, 2048), BF16),
-        in_specs=[vmem] * 7 + [anywhere] * 2,
-        out_specs=vmem,
+        in_specs=[hbm] * 9,
+        out_specs=pl.BlockSpec(memory_space=pltpu.VMEM),
         scratch_shapes=scratch,
         compiler_params=pltpu.CompilerParams(
             collective_id=0, has_side_effects=True, vmem_limit_bytes=48 * 1024 * 1024
         ),
     )(
-        query, keys, values, gate_logit.T, beta_logit.T, decay_rate.reshape(NH, 1),
+        query, keys, values, gate_logit.T, beta_logit.T, decay_rate.reshape(1, NH),
         norm_gain.reshape(1, BLK), gate_z, out_weight,
     )
 

time: 80.4 us -> 55.4 us (0.69)
  the two profiles are of different devices: /device:TPU:24 before, /device:TPU:60 now
where the time goes in v2:
time: 55.4 us; the launch traced here: 55 us
  Pallas kernels  46 us (83%)
  local copies, waits for them, and re-layouts  8.98 us (16%)
    pallas_call x1, Pallas kernels, on_device(): pl.pallas_call(kernel, out_shape=jax.ShapeDtypeStruct((64, 2048), BF16),...  46 us
    unnamed x19, local copies, waits for them, and re-layouts  8.98 us

profile of v2, /device:TPU:60, one launch (start us, length us, event | category | flops | bytes accessed | tf_op | source)
XLA Modules:
  0.0 55.0 jit_solution(14625412444264840354)
XLA Ops:
  0.0 0.0 copy-start
  0.0 1.6 %copy-done = bf16[512,2048]{1,0:T(8,128)(2,1)S(1)} copy-done((bf16[512,2048]{1,0:T(8,128)(2,1)S(1)}, bf16[512,2048]{1,0:T(8,128)(2,1)}, u32[]{:S(2)}) %copy-start) | copy-done | bytes 2097176
  1.6 0.0 copy-start.1
  1.6 1.0 %copy-done.1 = bf16[512,512]{1,0:T(8,128)(2,1)S(1)} copy-done((bf16[512,512]{1,0:T(8,128)(2,1)S(1)}, bf16[512,512]{1,0:T(8,128)(2,1)}, u32[]{:S(2)}) %copy-start.1) | copy-done | bytes 524312
  2.6 0.0 copy-start.2
  2.6 1.0 %copy-done.2 = bf16[512,512]{1,0:T(8,128)(2,1)S(1)} copy-done((bf16[512,512]{1,0:T(8,128)(2,1)S(1)}, bf16[512,512]{1,0:T(8,128)(2,1)}, u32[]{:S(2)}) %copy-start.2) | copy-done | bytes 524312
  3.7 0.0 copy-start.3
  3.7 0.9 %copy-done.3 = bf16[512,256]{1,0:T(8,128)(2,1)S(1)} copy-done((bf16[512,256]{1,0:T(8,128)(2,1)S(1)}, bf16[512,256]{1,0:T(8,128)(2,1)}, u32[]{:S(2)}) %copy-start.3) | copy-done | bytes 262168
  4.6 0.0 copy-start.4
  4.6 0.9 %copy-done.4 = bf16[512,256]{1,0:T(8,128)(2,1)S(1)} copy-done((bf16[512,256]{1,0:T(8,128)(2,1)S(1)}, bf16[512,256]{1,0:T(8,128)(2,1)}, u32[]{:S(2)}) %copy-start.4) | copy-done | bytes 262168
  5.6 0.0 copy-start.5
  5.6 0.7 %copy-done.5 = f32[512,4]{0,1:T(4,128)S(1)} copy-done((f32[512,4]{0,1:T(4,128)S(1)}, f32[512,4]{0,1:T(4,128)}, u32[]{:S(2)}) %copy-start.5) | copy-done | bytes 8216
  6.3 0.0 copy-start.6
  6.3 0.7 %copy-done.6 = f32[512,4]{0,1:T(4,128)S(1)} copy-done((f32[512,4]{0,1:T(4,128)S(1)}, f32[512,4]{0,1:T(4,128)}, u32[]{:S(2)}) %copy-start.6) | copy-done | bytes 8216
  7.0 0.0 copy-start.7
  7.0 0.7 %copy-done.7 = f32[4]{0:T(128)S(1)} copy-done((f32[4]{0:T(128)S(1)}, f32[4]{0:T(128)}, u32[]{:S(2)}) %copy-start.7) | copy-done | bytes 40
  7.6 0.0 copy-start.8
  7.6 0.7 %copy-done.8 = f32[128]{0:T(128)S(1)} copy-done((f32[128]{0:T(128)S(1)}, f32[128]{0:T(128)}, u32[]{:S(2)}) %copy-start.8) | copy-done | bytes 536
  8.3 46.0 %shard_map.91 = bf16[64,2048]{1,0:T(8,128)(2,1)S(1)} custom-call(bf16[512,256]{1,0:T(8,128)(2,1)S(1)} %copy-done.3, bf16[512,256]{1,0:T(8,128)(2,1)S(1)} %copy-done.4, bf16[512,512]{1,0:T(8,128)(2,1)S(1)} %copy-done.1, f32[4,512]{1,0:T(4,128)S(1)} %bitcast.4, f32[4,512]{1,0:T(4,128)S(1)} %bitcast.5, f32[1,4]{1,0:T(1,128)S(1)} %bitcast.6, ...), custom_call_target="tpu_custom_call" | custom-call | tf_op jit(solution)/shard_map/pallas_call | solution.py:481
  54.3 0.7 %copy.11 = bf16[64,2048]{1,0:T(8,128)(2,1)} copy(bf16[64,2048]{1,0:T(8,128)(2,1)S(1)} %shard_map.91) | data formatting | bytes 524288
Async XLA Ops:
  0.0 1.6 %copy-start = (bf16[512,2048]{1,0:T(8,128)(2,1)S(1)}, bf16[512,2048]{1,0:T(8,128)(2,1)}, u32[]{:S(2)}) copy-start(bf16[512,2048]{1,0:T(8,128)(2,1)} %w_hbm.1) | copy-start | bytes 6291460
  1.6 1.0 %copy-start.1 = (bf16[512,512]{1,0:T(8,128)(2,1)S(1)}, bf16[512,512]{1,0:T(8,128)(2,1)}, u32[]{:S(2)}) copy-start(bf16[512,512]{1,0:T(8,128)(2,1)} %v_hbm.1) | copy-start | bytes 1572868
  2.6 1.0 %copy-start.2 = (bf16[512,512]{1,0:T(8,128)(2,1)S(1)}, bf16[512,512]{1,0:T(8,128)(2,1)}, u32[]{:S(2)}) copy-start(bf16[512,512]{1,0:T(8,128)(2,1)} %z_hbm.1) | copy-start | bytes 1572868
  3.7 0.9 %copy-start.3 = (bf16[512,256]{1,0:T(8,128)(2,1)S(1)}, bf16[512,256]{1,0:T(8,128)(2,1)}, u32[]{:S(2)}) copy-start(bf16[512,256]{1,0:T(8,128)(2,1)} %q_hbm.1) | copy-start | bytes 786436
  4.6 0.9 %copy-start.4 = (bf16[512,256]{1,0:T(8,128)(2,1)S(1)}, bf16[512,256]{1,0:T(8,128)(2,1)}, u32[]{:S(2)}) copy-start(bf16[512,256]{1,0:T(8,128)(2,1)} %k_hbm.1) | copy-start | bytes 786436
  5.6 0.7 %copy-start.5 = (f32[512,4]{0,1:T(4,128)S(1)}, f32[512,4]{0,1:T(4,128)}, u32[]{:S(2)}) copy-start(f32[512,4]{0,1:T(4,128)} %param.12) | copy-start | bytes 24580
  6.3 0.7 %copy-start.6 = (f32[512,4]{0,1:T(4,128)S(1)}, f32[512,4]{0,1:T(4,128)}, u32[]{:S(2)}) copy-start(f32[512,4]{0,1:T(4,128)} %param.13) | copy-start | bytes 24580
  7.0 0.7 %copy-start.7 = (f32[4]{0:T(128)S(1)}, f32[4]{0:T(128)}, u32[]{:S(2)}) copy-start(f32[4]{0:T(128)} %param.14) | copy-start | bytes 52
  7.6 0.7 %copy-start.8 = (f32[128]{0:T(128)S(1)}, f32[128]{0:T(128)}, u32[]{:S(2)}) copy-start(f32[128]{0:T(128)} %param.15) | copy-start | bytes 1540

commit v3 on v2

--- a/solution.py
+++ b/solution.py
@@ -14,9 +14,8 @@
 ROWS_D = 128
 ROWS_C = 144
 ROWS_M = 272
-TREE = (
-    (0, 0, None), (4, 0, 12), (2, 0, 8), (1, 0, 0), (6, 4, 10), (5, 4, 4), (3, 2, 2), (7, 6, 6),
-)
+PREFIXES = ((8, 2, 14), (12, 4, 15), (12, 10, 16), (16, 6, 17))
+BEFORE = (None, 0, 8, 14, 12, 15, 16, 17)
 F32 = jnp.float32
 BF16 = jnp.bfloat16
 
@@ -86,72 +85,58 @@
         s["cols"][b] = s["rows"][b].T
 
 
-def block_terms(k_ref, q_ref, v_ref, s):
+def block_terms(kh, k_ref, q_ref, v_ref, s):
     row_ids = lax.broadcasted_iota(jnp.int32, (BLK, BLK), 0)
     col_ids = lax.broadcasted_iota(jnp.int32, (BLK, BLK), 1)
     inclusive = col_ids <= row_ids
     differ = row_ids ^ col_ids
     ident = jnp.where(row_ids == col_ids, 1.0, 0.0)
-
-    def group(g, carry):
-        lower = {}
-        for i in range(2):
-            b = 2 * g + i
-            tok = pl.ds(pl.multiple_of(b * BLK, BLK), BLK)
-            cols = s["cols"][b]
-            for kh in range(2):
-                kt = s["kt"][2 * b + kh]
-                kk = dot(k_ref[tok, BLK * kh : BLK * (kh + 1)], kt)
-                qk = dot(q_ref[tok, BLK * kh : BLK * (kh + 1)], kt)
-                rk = s["rows"][b, pl.ds(24 + 2 * kh, 1), :]
-                for h in (2 * kh, 2 * kh + 1):
-                    gap = cols[:, h : h + 1] - s["rows"][b, pl.ds(h, 1), :]
-                    ratio = jnp.exp(jnp.where(inclusive, gap, -1e30)) * rk
-                    s["mix"][4 * b + h] = (ratio * qk).astype(BF16)
-                    lower[i, h] = cols[:, 4 + h : 5 + h] * ratio * kk
-                    s["low"][4 * i + h] = lower[i, h]
-        pairs = [(i, h) for i in range(2) for h in range(NH)]
-        for p in pairs:
-            off = jnp.where(differ == 1, s["low"][4 * p[0] + p[1]], 0.0)
-            s["inv"][4 * p[0] + p[1]] = ident - off
-        for level in range(1, 7):
-            here = (differ >> level) == 1
-            part = {}
-            for p in pairs:
-                n = 4 * p[0] + p[1]
-                off = jnp.where(here, s["low"][n], 0.0).astype(BF16)
-                part[p] = dot(off, s["inv"][n].astype(BF16)).astype(BF16)
-            for p in pairs:
-                n = 4 * p[0] + p[1]
-                inv = s["inv"][n]
-                s["inv"][n] = inv - dot(inv.astype(BF16), part[p])
-        for i, h in pairs:
-            b = 2 * g + i
-            tok = pl.ds(pl.multiple_of(b * BLK, BLK), BLK)
-            inv = s["inv"][4 * i + h]
-            t_v = (inv * s["rows"][b, pl.ds(16 + h, 1), :]).astype(BF16)
-            t_k = (inv * s["rows"][b, pl.ds(20 + h, 1), :]).astype(BF16)
-            kh = h // 2
-            s["upd"][4 * b + h] = dot(t_v, v_ref[tok, BLK * h : BLK * (h + 1)])
-            s["wts"][4 * b + h] = dot(t_k, k_ref[tok, BLK * kh : BLK * (kh + 1)]).astype(BF16)
-        return carry
-
-    lax.fori_loop(0, NB // 2, group, 0)
-
-
-def run_shard(s):
-    row_ids = lax.broadcasted_iota(jnp.int32, (BLK, BLK), 0)
-    col_ids = lax.broadcasted_iota(jnp.int32, (BLK, BLK), 1)
-    eye = row_ids == col_ids
-    for h in range(NH):
-        s["state"][h, :, :BLK] = jnp.zeros((BLK, BLK), F32)
-        s["state"][h, :, BLK:] = jnp.where(eye, 1.0, 0.0)
-
-    def block(b, carry):
+    key_lanes = slice(BLK * kh, BLK * (kh + 1))
+    pairs = [(b, h) for b in range(NB) for h in (2 * kh, 2 * kh + 1)]
+    for b in range(NB):
+        tok = pl.ds(b * BLK, BLK)
         cols = s["cols"][b]
-        for h in range(NH):
+        kt = s["kt"][2 * b + kh]
+        kk = dot(k_ref[tok, key_lanes], kt)
+        qk = dot(q_ref[tok, key_lanes], kt)
+        rk = s["rows"][b, pl.ds(24 + 2 * kh, 1), :]
+        for h in (2 * kh, 2 * kh + 1):
+            gap = cols[:, h : h + 1] - s["rows"][b, pl.ds(h, 1), :]
+            ratio = jnp.exp(jnp.where(inclusive, gap, -1e30)) * rk
+            s["mix"][4 * b + h] = (ratio * qk).astype(BF16)
+            low = cols[:, 4 + h : 5 + h] * ratio * kk
+            s["low"][2 * b + h % 2] = low
+            s["inv"][2 * b + h % 2] = ident - jnp.where(differ == 1, low, 0.0)
+    for level in range(1, 7):
+        here = (differ >> level) == 1
+        part = {}
+        for b, h in pairs:
+            n = 2 * b + h % 2
+            off = jnp.where(here, s["low"][n], 0.0).astype(BF16)
+            part[n] = dot(off, s["inv"][n].astype(BF16)).astype(BF16)
+        for b, h in pairs:
+            n = 2 * b + h % 2
+            inv = s["inv"][n]
+            s["inv"][n] = inv - dot(inv.astype(BF16), part[n])
+    for b, h in pairs:
+        tok = pl.ds(b * BLK, BLK)
+        inv = s["inv"][2 * b + h % 2]
+        t_v = (inv * s["rows"][b, pl.ds(16 + h, 1), :]).astype(BF16)
+        t_k = (inv * s["rows"][b, pl.ds(20 + h, 1), :]).astype(BF16)
+        s["upd"][4 * b + h] = dot(t_v, v_ref[tok, BLK * h : BLK * (h + 1)])
+        s["wts"][4 * b + h] = dot(t_k, k_ref[tok, key_lanes]).astype(BF16)
+
+
+def run_shard(kh, s):
+    heads = (2 * kh, 2 * kh + 1)
+    row_ids = lax.broadcasted_iota(jnp.int32, (BLK, 2 * BLK), 0)
+    col_ids = lax.broadcasted_iota(jnp.int32, (BLK, 2 * BLK), 1)
+    states = {h: jnp.where(row_ids + BLK == col_ids, 1.0, 0.0) for h in heads}
+    for b in range(NB):
+        cols = s["cols"][b]
+        for h in heads:
             n = 4 * b + h
-            state = s["state"][h].astype(BF16)
+            state = states[h].astype(BF16)
             s["sb"][n] = state
             ws = dot(s["wts"][n], state)
             res_s = s["upd"][n] - ws[:, :BLK]
@@ -161,14 +146,11 @@
             s["rb"][n, :, BLK:] = res_a.astype(BF16)
             s["re"][h, :, :BLK] = (end * res_s).astype(BF16)
             s["re"][h, :, BLK:] = (end * res_a).astype(BF16)
-        for h in range(NH):
+        for h in heads:
             gain = s["rows"][b, pl.ds(28 + h, 1), :]
-            grow = dot(s["kt"][2 * b + h // 2], s["re"][h])
-            s["state"][h, :, :BLK] = gain * s["state"][h, :, :BLK] + grow[:, :BLK]
-            s["state"][h, :, BLK:] = gain * s["state"][h, :, BLK:] + grow[:, BLK:]
-        return carry
-
-    lax.fori_loop(0, NB, block, 0)
+            grow = dot(s["kt"][2 * b + kh], s["re"][h])
+            states[h] = jnp.concatenate([gain, gain], axis=1) * states[h] + grow
+    return states
 
 
 def write_message(ref, c, fix, inject):
@@ -211,7 +193,7 @@
 def kernel(
     q_hbm, k_hbm, v_hbm, gl_hbm, bl_hbm, rate_hbm, gain_hbm, z_hbm, w_hbm, out_ref,
     q_ref, k_ref, v_ref, gl_ref, bl_ref, rate_ref, gain_ref, z_buf, w_buf,
-    g16, rows, cols, rq, kt, mix, low, inv, upd, wts, state, sb, rb, re, msg, oloc, corr,
+    g16, rows, cols, rq, kt, mix, low, inv, upd, wts, sb, rb, re, msg, oloc, corr,
     gate, parts, rmsg, rowbuf, start, xst, xin,
     gated, parta, recva, partb, sumb, relay, hop, recvb,
     load_sem, m_send, m_recv, r_send, r_recv, x_send, x_recv,
@@ -219,7 +201,7 @@
 ):
     s = dict(
         g16=g16, rows=rows, cols=cols, rq=rq, kt=kt, mix=mix, low=low, inv=inv, upd=upd, wts=wts,
-        state=state, sb=sb, rb=rb, re=re, msg=msg, oloc=oloc, corr=corr,
+        sb=sb, rb=rb, re=re, msg=msg, oloc=oloc, corr=corr,
     )
     loads = [
         pltpu.make_async_copy(src, dst, load_sem.at[i])
@@ -263,9 +245,6 @@
         load.wait()
 
     gates(gl_ref, bl_ref, rate_ref, k_ref, q_ref, s)
-    block_terms(k_ref, q_ref, v_ref, s)
-    run_shard(s)
-    pl.semaphore_wait(barrier, len(peers))
     sends = []
 
     def go(copy):
@@ -274,21 +253,26 @@
 
     row_ids = lax.broadcasted_iota(jnp.int32, (BLK, BLK), 0)
     eye = row_ids == lax.broadcasted_iota(jnp.int32, (BLK, BLK), 1)
-    for h in range(NH):
-        total = g16[pl.ds(h, 1), :]
-        for b in range(1, NB):
-            total = total + g16[pl.ds(4 * b + h, 1), :]
-        c = jnp.exp(jnp.broadcast_to(total[:, BLK - 1 : BLK], (1, BLK)))
-        fix = jnp.where(eye, c, 0.0) - state[h, :, BLK:]
-        write_message(msg.at[h], c, fix.T, state[h, :, :BLK].T)
-
-        @pl.when(z != 2 * h + core)
-        def _():
-            remote(msg.at[h], parts.at[z], m_send.at[h], m_recv.at[z], owner(h)).start()
-
-        @pl.when(z == 2 * h + core)
-        def _():
-            parts[z] = msg[h]
+    for kh in range(2):
+        block_terms(kh, k_ref, q_ref, v_ref, s)
+        states = run_shard(kh, s)
+        if kh == 0:
+            pl.semaphore_wait(barrier, len(peers))
+        for h in (2 * kh, 2 * kh + 1):
+            total = g16[pl.ds(h, 1), :]
+            for b in range(1, NB):
+                total = total + g16[pl.ds(4 * b + h, 1), :]
+            c = jnp.exp(jnp.broadcast_to(total[:, BLK - 1 : BLK], (1, BLK)))
+            fix = jnp.where(eye, c, 0.0) - states[h][:, BLK:]
+            write_message(msg.at[h], c, fix.T, states[h][:, :BLK].T)
+
+            @pl.when(z != 2 * h + core)
+            def _():
+                remote(msg.at[h], parts.at[z], m_send.at[h], m_recv.at[z], owner(h)).start()
+
+            @pl.when(z == 2 * h + core)
+            def _():
+                parts[z] = msg[h]
 
     for b in range(NB):
         block_output(b, q_ref, s)
@@ -318,6 +302,8 @@
             def _():
                 remote(rmsg, rowbuf.at[y], r_send.at[i - 1], r_recv.at[y], at((y + i) % NY, z)).start()
 
+        for first, second, out in PREFIXES:
+            compose(parts.at[first], parts.at[second], parts.at[out])
         start[...] = jnp.zeros_like(start)
         for r in range(NY - 1):
 
@@ -329,11 +315,10 @@
                 else:
                     start[...] = step(rowbuf.at[r], start[...])
 
-        states = {0: start[...]}
-        for j, source, stretch in TREE:
-            if stretch is not None:
-                states[j] = step(parts.at[stretch], states[source])
-            xst[j] = states[j].astype(BF16)
+        row_state = start[...]
+        for j, stretch in enumerate(BEFORE):
+            at_shard = row_state if stretch is None else step(parts.at[stretch], row_state)
+            xst[j] = at_shard.astype(BF16)
 
             @pl.when(j != z)
             def _():
@@ -448,7 +433,6 @@
         pltpu.VMEM((8, BLK, BLK), F32),
         pltpu.VMEM((pairs, BLK, BLK), F32),
         pltpu.VMEM((pairs, BLK, BLK), BF16),
-        pltpu.VMEM((NH, BLK, 2 * BLK), F32),
         pltpu.VMEM((pairs, BLK, 2 * BLK), BF16),
         pltpu.VMEM((pairs, BLK, 2 * BLK), BF16),
         pltpu.VMEM((NH, BLK, 2 * BLK), BF16),
@@ -456,7 +440,7 @@
         pltpu.VMEM((NH, 512, BLK), F32),
         pltpu.VMEM((NH, 512, BLK), BF16),
         pltpu.VMEM((512, 512), F32),
-        pltpu.VMEM((14, ROWS_M, BLK), BF16),
+        pltpu.VMEM((18, ROWS_M, BLK), BF16),
         pltpu.VMEM((ROWS_M, BLK), BF16),
         pltpu.VMEM((NY, ROWS_M, BLK), BF16),
         pltpu.VMEM((BLK, BLK), F32),
@@ -485,7 +469,7 @@
         out_specs=pl.BlockSpec(memory_space=pltpu.VMEM),
         scratch_shapes=scratch,
         compiler_params=pltpu.CompilerParams(
-            collective_id=0, has_side_effects=True, vmem_limit_bytes=48 * 1024 * 1024
+            collective_id=0, has_side_effects=True, vmem_limit_bytes=56 * 1024 * 1024
         ),
     )(
         query, keys, values, gate_logit.T, beta_logit.T, decay_rate.reshape(1, NH),

time: 55.4 us -> 48.6 us (0.88)
  local copies, waits for them, and re-layouts: 8.98 us -> 1.67 us
  Pallas kernels: 46 us -> 46.6 us
    unnamed x19 -> x1, local copies, waits for them, and re-layouts: 8.98 us -> 1.67 us
    pallas_call x1, Pallas kernels: 46 us -> 46.6 us  [on_device(): pl.pallas_call(kernel, out_shape=jax.ShapeDtypeStruct((64, 2048), BF16),...]
where the time goes in v3:
time: 48.6 us; the launch traced here: 48.3 us
  Pallas kernels  46.6 us (96%)
  local copies, waits for them, and re-layouts  1.67 us (3%)
    pallas_call x1, Pallas kernels, on_device(): pl.pallas_call(kernel, out_shape=jax.ShapeDtypeStruct((64, 2048), BF16),...  46.6 us
    unnamed x1, local copies, waits for them, and re-layouts  1.67 us

profile of v3, /device:TPU:60, one launch (start us, length us, event | category | flops | bytes accessed | tf_op | source)
XLA Modules:
  0.0 48.3 jit_solution(450585330204335404)
XLA Ops:
  0.0 46.6 %shard_map.91 = bf16[64,2048]{1,0:T(8,128)(2,1)} custom-call(bf16[512,256]{1,0:T(8,128)(2,1)} %q_hbm.1, bf16[512,256]{1,0:T(8,128)(2,1)} %k_hbm.1, bf16[512,512]{1,0:T(8,128)(2,1)} %v_hbm.1, f32[4,512]{1,0:T(4,128)} %bitcast.4, f32[4,512]{1,0:T(4,128)} %bitcast.5, f32[1,4]{1,0:T(1,128)} %bitcast.6, f32[1,128]{1,0:T(1,128)} %bitcast.7, ...), custom_call_target="tpu_custom_call" | custom-call | tf_op jit(solution)/shard_map/pallas_call | solution.py:465
  46.6 1.7 %copy.11 = bf16[64,2048]{1,0:T(8,128)(2,1)} copy(bf16[64,2048]{1,0:T(8,128)(2,1)} %shard_map.91) | data formatting | bytes 524288

commit v4 on v3

--- a/solution.py
+++ b/solution.py
@@ -107,6 +107,7 @@
             low = cols[:, 4 + h : 5 + h] * ratio * kk
             s["low"][2 * b + h % 2] = low
             s["inv"][2 * b + h % 2] = ident - jnp.where(differ == 1, low, 0.0)
+        yield
     for level in range(1, 7):
         here = (differ >> level) == 1
         part = {}
@@ -114,10 +115,12 @@
             n = 2 * b + h % 2
             off = jnp.where(here, s["low"][n], 0.0).astype(BF16)
             part[n] = dot(off, s["inv"][n].astype(BF16)).astype(BF16)
+        yield
         for b, h in pairs:
             n = 2 * b + h % 2
             inv = s["inv"][n]
             s["inv"][n] = inv - dot(inv.astype(BF16), part[n])
+        yield
     for b, h in pairs:
         tok = pl.ds(b * BLK, BLK)
         inv = s["inv"][2 * b + h % 2]
@@ -127,11 +130,12 @@
         s["wts"][4 * b + h] = dot(t_k, k_ref[tok, key_lanes]).astype(BF16)
 
 
-def run_shard(kh, s):
+def run_shard(kh, states, s):
     heads = (2 * kh, 2 * kh + 1)
     row_ids = lax.broadcasted_iota(jnp.int32, (BLK, 2 * BLK), 0)
     col_ids = lax.broadcasted_iota(jnp.int32, (BLK, 2 * BLK), 1)
-    states = {h: jnp.where(row_ids + BLK == col_ids, 1.0, 0.0) for h in heads}
+    for h in heads:
+        states[h] = jnp.where(row_ids + BLK == col_ids, 1.0, 0.0)
     for b in range(NB):
         cols = s["cols"][b]
         for h in heads:
@@ -146,11 +150,12 @@
             s["rb"][n, :, BLK:] = res_a.astype(BF16)
             s["re"][h, :, :BLK] = (end * res_s).astype(BF16)
             s["re"][h, :, BLK:] = (end * res_a).astype(BF16)
+        yield
         for h in heads:
             gain = s["rows"][b, pl.ds(28 + h, 1), :]
             grow = dot(s["kt"][2 * b + kh], s["re"][h])
             states[h] = jnp.concatenate([gain, gain], axis=1) * states[h] + grow
-    return states
+        yield
 
 
 def write_message(ref, c, fix, inject):
@@ -253,12 +258,10 @@
 
     row_ids = lax.broadcasted_iota(jnp.int32, (BLK, BLK), 0)
     eye = row_ids == lax.broadcasted_iota(jnp.int32, (BLK, BLK), 1)
-    for kh in range(2):
-        block_terms(kh, k_ref, q_ref, v_ref, s)
-        states = run_shard(kh, s)
-        if kh == 0:
-            pl.semaphore_wait(barrier, len(peers))
-        for h in (2 * kh, 2 * kh + 1):
+    states = {}
+
+    def send_heads(heads):
+        for h in heads:
             total = g16[pl.ds(h, 1), :]
             for b in range(1, NB):
                 total = total + g16[pl.ds(4 * b + h, 1), :]
@@ -274,6 +277,18 @@
             def _():
                 parts[z] = msg[h]
 
+    for _ in block_terms(0, k_ref, q_ref, v_ref, s):
+        pass
+    second = block_terms(1, k_ref, q_ref, v_ref, s)
+    for _ in run_shard(0, states, s):
+        next(second)
+    pl.semaphore_wait(barrier, len(peers))
+    send_heads((0, 1))
+    for _ in second:
+        pass
+    for _ in run_shard(1, states, s):
+        pass
+    send_heads((2, 3))
     for b in range(NB):
         block_output(b, q_ref, s)
     for load in loads[6:]:
@@ -334,7 +349,7 @@
         def _():
             remote(xst.at[0], xin.at[h], x_send.at[0], x_recv.at[h], at(y, z)).wait_recv()
 
-    def gate_half(which):
+    def gate_half(which, slot):
         for h in range(NH):
             for j in range(NX):
                 tok = pl.ds(pl.multiple_of((2 * j + which) * 64, 64), 64)
@@ -343,14 +358,16 @@
                 mean = jnp.mean(core_out * core_out, axis=1, keepdims=True)
                 scale = r * lax.rsqrt(r * r * mean + 1e-06)
                 lanes = slice(BLK * h, BLK * (h + 1))
-                gated[64 * j : 64 * (j + 1), lanes] = (core_out * scale * gate[tok, lanes]).astype(BF16)
+                gated[slot, 64 * j : 64 * (j + 1), lanes] = (core_out * scale * gate[tok, lanes]).astype(BF16)
 
     order = (0, 2, 1, 3)
-    gate_half(1 - core)
-    for n in order:
-        parta[n] = dot(gated[...], w_buf[:, 512 * n : 512 * (n + 1)]).astype(BF16)
+    def send_over(n):
+        parta[n] = dot(gated[0], w_buf[:, 512 * n : 512 * (n + 1)]).astype(BF16)
         go(remote(parta.at[n], recva.at[n], a_send.at[n], a_recv.at[n], on_line(x, 1 - core)))
-    gate_half(core)
+
+    gate_half(1 - core, 0)
+    send_over(order[0])
+    gate_half(core, 1)
 
     def rows_of(chip):
         return pl.ds(pl.multiple_of(64 * chip, 64), 64)
@@ -366,7 +383,9 @@
 
     for count, n in enumerate(order):
         onward, back = ways(n)
-        partb[n] = dot(gated[...], w_buf[:, 512 * n : 512 * (n + 1)])
+        if count < 3:
+            send_over(order[count + 1])
+        partb[n] = dot(gated[1], w_buf[:, 512 * n : 512 * (n + 1)])
         remote(parta.at[n], recva.at[n], a_send.at[n], a_recv.at[n], on_line(x, core)).wait_recv()
         partb[n] = partb[n] + recva[n].astype(F32)
         sumb[n] = partb[n].astype(BF16)
@@ -446,7 +465,7 @@
         pltpu.VMEM((BLK, BLK), F32),
         pltpu.VMEM((NZ, BLK, BLK), BF16),
         pltpu.VMEM((NH, BLK, BLK), BF16),
-        pltpu.VMEM((256, 512), BF16),
+        pltpu.VMEM((2, 256, 512), BF16),
         pltpu.VMEM((4, 256, 512), BF16),
         pltpu.VMEM((4, 256, 512), BF16),
         pltpu.VMEM((4, 256, 512), F32),

time: 48.6 us -> 47.1 us (0.969)
  Pallas kernels: 46.6 us -> 45.1 us
    pallas_call x1, Pallas kernels: 46.6 us -> 45.1 us  [on_device(): pl.pallas_call(kernel, out_shape=jax.ShapeDtypeStruct((64, 2048), BF16),...]
where the time goes in v4:
time: 47.1 us; the launch traced here: 46.7 us
  Pallas kernels  45.1 us (96%)
  local copies, waits for them, and re-layouts  1.67 us (4%)
    pallas_call x1, Pallas kernels, on_device(): pl.pallas_call(kernel, out_shape=jax.ShapeDtypeStruct((64, 2048), BF16),...  45.1 us
    unnamed x1, local copies, waits for them, and re-layouts  1.67 us

profile of v4, /device:TPU:60, one launch (start us, length us, event | category | flops | bytes accessed | tf_op | source)
XLA Modules:
  0.0 46.7 jit_solution(14223908651508497071)
XLA Ops:
  0.0 45.1 %shard_map.91 = bf16[64,2048]{1,0:T(8,128)(2,1)} custom-call(bf16[512,256]{1,0:T(8,128)(2,1)} %q_hbm.1, bf16[512,256]{1,0:T(8,128)(2,1)} %k_hbm.1, bf16[512,512]{1,0:T(8,128)(2,1)} %v_hbm.1, f32[4,512]{1,0:T(4,128)} %bitcast.4, f32[4,512]{1,0:T(4,128)} %bitcast.5, f32[1,4]{1,0:T(1,128)} %bitcast.6, f32[1,128]{1,0:T(1,128)} %bitcast.7, ...), custom_call_target="tpu_custom_call" | custom-call | tf_op jit(solution)/shard_map/pallas_call | solution.py:484
  45.1 1.7 %copy.11 = bf16[64,2048]{1,0:T(8,128)(2,1)} copy(bf16[64,2048]{1,0:T(8,128)(2,1)} %shard_map.91) | data formatting | bytes 524288

commit v5 on v4

--- a/solution.py
+++ b/solution.py
@@ -350,15 +350,19 @@
             remote(xst.at[0], xin.at[h], x_send.at[0], x_recv.at[h], at(y, z)).wait_recv()
 
     def gate_half(which, slot):
+        toks = [pl.ds(pl.multiple_of((2 * j + which) * 64, 64), 64) for j in range(NX)]
+
+        def rows_for(part):
+            return jnp.concatenate([part(tok) for tok in toks], axis=0)
+
         for h in range(NH):
-            for j in range(NX):
-                tok = pl.ds(pl.multiple_of((2 * j + which) * 64, 64), 64)
-                core_out = oloc[h, tok, :] + dot_nt(corr[h, tok, :], xin[h])
-                r = rq[h // 2, tok, :]
-                mean = jnp.mean(core_out * core_out, axis=1, keepdims=True)
-                scale = r * lax.rsqrt(r * r * mean + 1e-06)
-                lanes = slice(BLK * h, BLK * (h + 1))
-                gated[slot, 64 * j : 64 * (j + 1), lanes] = (core_out * scale * gate[tok, lanes]).astype(BF16)
+            lanes = slice(BLK * h, BLK * (h + 1))
+            core_out = rows_for(lambda tok: oloc[h, tok, :])
+            core_out = core_out + dot_nt(rows_for(lambda tok: corr[h, tok, :]), xin[h])
+            r = rows_for(lambda tok: rq[h // 2, tok, :])
+            mean = jnp.mean(core_out * core_out, axis=1, keepdims=True)
+            scale = r * lax.rsqrt(r * r * mean + 1e-06)
+            gated[slot, :, lanes] = (core_out * scale * rows_for(lambda tok: gate[tok, lanes])).astype(BF16)
 
     order = (0, 2, 1, 3)
     def send_over(n):

time: 47.1 us -> 47 us (level)
  no operation moved by 1% of the time
where the time goes in v5:
time: 47 us; the launch traced here: 46.6 us
  Pallas kernels  44.9 us (96%)
  local copies, waits for them, and re-layouts  1.67 us (4%)
    pallas_call x1, Pallas kernels, on_device(): pl.pallas_call(kernel, out_shape=jax.ShapeDtypeStruct((64, 2048), BF16),...  44.9 us
    unnamed x1, local copies, waits for them, and re-layouts  1.67 us

profile of v5, /device:TPU:60, one launch (start us, length us, event | category | flops | bytes accessed | tf_op | source)
XLA Modules:
  0.0 46.6 jit_solution(9575639131257536181)
XLA Ops:
  0.0 44.9 %shard_map.91 = bf16[64,2048]{1,0:T(8,128)(2,1)} custom-call(bf16[512,256]{1,0:T(8,128)(2,1)} %q_hbm.1, bf16[512,256]{1,0:T(8,128)(2,1)} %k_hbm.1, bf16[512,512]{1,0:T(8,128)(2,1)} %v_hbm.1, f32[4,512]{1,0:T(4,128)} %bitcast.4, f32[4,512]{1,0:T(4,128)} %bitcast.5, f32[1,4]{1,0:T(1,128)} %bitcast.6, f32[1,128]{1,0:T(1,128)} %bitcast.7, ...), custom_call_target="tpu_custom_call" | custom-call | tf_op jit(solution)/shard_map/pallas_call | solution.py:488
  44.9 1.7 %copy.11 = bf16[64,2048]{1,0:T(8,128)(2,1)} copy(bf16[64,2048]{1,0:T(8,128)(2,1)} %shard_map.91) | data formatting | bytes 524288
